TPU v7x, 32 devices: a whole 2x2x4 slice. The times are simulated.
32 devices in a mesh: frame: 16 (over z, y, x), row: 2 (over core).
Axes of the slice: x: 2, y: 2, z: 4, core: 2. Of those that a mesh axis runs over, the one named last changes fastest.
Arguments:
- latents: bfloat16 [32, 16, 36, 320], P('frame', 'row'), may hold values from -6 to 6
- conv_first: bfloat16 [3, 3, 320, 320], replicated, may hold values from -0.109375 to 0.109375
- conv_second: bfloat16 [3, 3, 320, 320], replicated, may hold values from -0.109375 to 0.109375
- conv_time: bfloat16 [3, 320, 320], replicated, may hold values from -0.1875 to 0.1875
- cond_start: float32 [320], replicated, may hold values from -4 to 4
- cond_end: float32 [320], replicated, may hold values from -4 to 4
Outputs:
- blended: bfloat16 [32, 16, 36, 320], P('frame', 'row')
All inputs are finite; a program needn't handle non-finite values.
Results may differ from a plain program's by a relative error of at most 0.0047.
Values may be sent and summed in bfloat16 or wider, within the bound.
No kernel may reach another device: no remote copies, remote signals or barrier semaphores. Data moves between devices by JAX's collectives and lax.ppermute only.
A program may use at most 64 MiB of HBM per device.

v0:
```python
import jax
import jax.numpy as jnp
from jax import lax
from jax.sharding import PartitionSpec as P


def with_halo(block, sides, width):
    for axis, dim in sides:
        count = lax.axis_size(axis)
        forward = [(i, i + 1) for i in range(count - 1)]
        backward = [(target, source) for source, target in forward]
        low = lax.ppermute(
            lax.slice_in_dim(block, block.shape[dim] - width, None, axis=dim), axis, forward
        )
        high = lax.ppermute(lax.slice_in_dim(block, 0, width, axis=dim), axis, backward)
        block = jnp.concatenate([low, block, high], axis=dim)
    return block


def spatial(padded, weight):
    rows_n = padded.shape[-3] - 2
    cols_n = padded.shape[-2]
    widened = jnp.pad(padded, [(0, 0)] * (padded.ndim - 2) + [(1, 1), (0, 0)])
    total = None
    for a in range(3):
        for b in range(3):
            window = widened[..., a : a + rows_n, b : b + cols_n, :]
            term = jnp.einsum(
                "...c,cd->...d", window, weight[a, b], preferred_element_type=jnp.float32
            )
            total = term if total is None else total + term
    return total


def temporal(padded, first_tap, mid_tap, last_tap):
    total = jnp.einsum("...c,cd->...d", padded[:-2], first_tap, preferred_element_type=jnp.float32)
    total = total + jnp.einsum(
        "...c,cd->...d", padded[1:-1], mid_tap, preferred_element_type=jnp.float32
    )
    total = total + jnp.einsum(
        "...c,cd->...d", padded[2:], last_tap, preferred_element_type=jnp.float32
    )
    return total


def shards(latents, conv_first, conv_second, conv_time, cond_start, cond_end):
    local_rows = latents.shape[1]
    video_deep = with_halo(latents, (("row", 1),), 2)
    shared = spatial(video_deep, conv_first)
    total_rows = lax.axis_size("row") * local_rows
    global_row = lax.axis_index("row") * local_rows - 1 + lax.iota(jnp.int32, local_rows + 2)
    inside = ((global_row >= 0) & (global_row < total_rows)).astype(jnp.float32)[
        None, None, :, None, None
    ]
    paired_pad = (
        jnp.stack([jax.nn.silu(shared + cond_start), jax.nn.silu(shared + cond_end)]) * inside
    ).astype(jnp.bfloat16)
    resid = (latents.astype(jnp.float32)[None] + spatial(paired_pad, conv_second)).astype(
        jnp.bfloat16
    )
    resid_pad = with_halo(jnp.moveaxis(resid, 0, 1), (("frame", 0),), 1)
    mixed_fwd = temporal(resid_pad[:, 0], conv_time[0], conv_time[1], conv_time[2])
    mixed_rev = temporal(resid_pad[:, 1], conv_time[2], conv_time[1], conv_time[0])
    forward = resid[0].astype(jnp.float32) + jax.nn.silu(mixed_fwd)
    returned = resid[1].astype(jnp.float32) + jax.nn.silu(mixed_rev)
    return (0.5 * (forward + returned)).astype(jnp.bfloat16)


def solution(mesh):
    placed = (P("frame", "row", None, None), P(), P(), P(), P(), P())
    return jax.shard_map(
        shards, mesh=mesh, in_specs=placed, out_specs=P("frame", "row", None, None), check_vma=False
    )
```

profile of v0, /device:TPU:0, one launch (start us, length us, event | category | flops | bytes accessed | tf_op | source)
XLA Modules:
  0.0 55.3 jit_solution(16846907320649877836)
XLA Ops:
  0.0 1.1 %copy.8 = bf16[2,8,36,320]{3,2,1,0:T(8,128)(2,1)S(1)} copy(bf16[2,8,36,320]{3,1,2,0:T(8,128)(2,1)} %param.6) | data formatting | bytes 737280 | tf_op args[0]
  1.2 1.3 %collective-permute-start.1 = (bf16[2,2,36,320]{3,2,1,0:T(8,128)(2,1)S(1)}, bf16[2,2,36,320]{3,2,1,0:T(8,128)(2,1)S(1)}, u32[]{:S(2)}, u32[]{:S(2)}) collective-permute-start(bf16[2,2,36,320]{3,2,1,0:T(8,128)(2,1)S(1)} %get-tuple-element.9), channel_id=1, source_target_pairs={{1,0},{3,2},{5,4},{7,6},{9,8},{11,10},{13,12},{15,14},{17,16},{19,... | collective-permute-start | bytes 276488 | tf_op jit(solution)/shard_map/ppermute | solution.py:15
  2.5 3.0 %collective-permute-start = (bf16[2,2,36,320]{3,2,1,0:T(8,128)(2,1)S(1)}, bf16[2,2,36,320]{3,2,1,0:T(8,128)(2,1)S(1)}, u32[]{:S(2)}, u32[]{:S(2)}) collective-permute-start(bf16[2,2,36,320]{3,2,1,0:T(8,128)(2,1)S(1)} %get-tuple-element.10), channel_id=1, source_target_pairs={{0,1},{2,3},{4,5},{6,7},{8,9},{10,11},{12,13},{14,15},{16,17},{18,... | collective-permute-start | bytes 276488 | tf_op jit(solution)/shard_map/ppermute | solution.py:12
  5.6 0.8 %collective-permute-done = bf16[2,2,36,320]{3,2,1,0:T(8,128)(2,1)S(1)} collective-permute-done((bf16[2,2,36,320]{3,2,1,0:T(8,128)(2,1)S(1)}, bf16[2,2,36,320]{3,2,1,0:T(8,128)(2,1)S(1)}, u32[]{:S(2)}, u32[]{:S(2)}) %collective-permute-start) | collective-permute-done | bytes 92192 | tf_op jit(solution)/shard_map/ppermute | solution.py:12
  6.7 1.7 %fusion.41 = f32[2,10,36,320]{3,2,1,0:T(8,128)S(1)} fusion(bf16[2,12,36,320]{3,2,1,0:T(8,128)(2,1)S(1)} %constant_dynamic-update-slice_fusion, bf16[3,3,320,320]{3,2,1,0:T(8,128)(2,1)} %param.7), kind=kOutput, calls=%fused_computation.50 | convolution fusion | flops 147456000 | bytes 1720320 | tf_op jit(solution)/shard_map/...c,cd->...d/dot_general | solution.py:28
  9.0 0.6 %fusion.37 = f32[2,10,36,320]{3,2,1,0:T(8,128)S(1)} fusion(bf16[2,12,36,320]{3,2,1,0:T(8,128)(2,1)S(1)} %constant_dynamic-update-slice_fusion, bf16[3,3,320,320]{3,2,1,0:T(8,128)(2,1)S(1)} %copy-done.3), kind=kOutput, calls=%fused_computation.46 | convolution fusion | flops 147456000 | bytes 1904640 | tf_op jit(solution)/shard_map/...c,cd->...d/dot_general | solution.py:28
  12.0 0.6 %fusion.25 = f32[2,10,36,320]{3,2,1,0:T(8,128)S(1)} fusion(bf16[2,8,36,320]{3,2,1,0:T(8,128)(2,1)S(1)} %copy.8, bf16[2,2,36,320]{3,2,1,0:T(8,128)(2,1)S(1)} %collective-permute-done, bf16[3,3,320,320]{3,2,1,0:T(8,128)(2,1)S(1)} %copy-done.3), kind=kOutput, calls=%fused_computation.34 | convolution fusion | flops 147686400 | bytes 1781760 | tf_op jit(solution)/shard_map/...c,cd->...d/dot_general | solution.py:28
  12.7 1.3 %multiply_bitcast_fusion.1 = (f32[1,2,10,36,320]{4,3,2,1,0:T(8,128)S(1)}, f32[1,2,10,36,320]{4,3,2,1,0:T(8,128)S(1)}) fusion(f32[320]{0:T(512)S(1)} %copy-done.4, f32[320]{0:T(512)S(1)} %copy-done.5, f32[2,10,36,320]{3,2,1,0:T(8,128)S(1)} %fusion.33, f32[2,10,36,320]{3,2,1,0:T(8,128)S(1)} %fusion.29, f32[2,10,36,320]{3,2,1,0:T(8,128)S(1)} %fusion.35, ...), kind=kOutput, calls=%fused_computation.16 | convolution fusion | flops 151603200 | bytes 12660736 | tf_op jit(solution)/shard_map/...c,cd->...d/dot_general | solution.py:28
  14.3 1.3 %copy-done.1 = bf16[3,3,320,320]{3,2,1,0:T(8,128)(2,1)S(1)} copy-done((bf16[3,3,320,320]{3,2,1,0:T(8,128)(2,1)S(1)}, bf16[3,3,320,320]{3,2,1,0:T(8,128)(2,1)}, u32[]{:S(2)}) %copy-start.1) | copy-done | bytes 1843224
  15.6 0.9 %fusion.21 = f32[2,2,8,36,320]{4,3,2,1,0:T(8,128)S(1)} fusion(bf16[2,2,10,36,320]{4,3,2,1,0:T(8,128)(2,1)S(1)} %fusion, bf16[3,3,320,320]{3,2,1,0:T(8,128)(2,1)S(1)} %copy-done.1), kind=kOutput, calls=%fused_computation.30 | convolution fusion | flops 235929600 | bytes 2949120 | tf_op jit(solution)/shard_map/...c,cd->...d/dot_general | solution.py:28
  16.5 0.9 %fusion.19 = f32[2,2,8,36,320]{4,3,2,1,0:T(8,128)S(1)} fusion(bf16[2,2,10,36,320]{4,3,2,1,0:T(8,128)(2,1)S(1)} %fusion, bf16[3,3,320,320]{3,2,1,0:T(8,128)(2,1)S(1)} %copy-done.1), kind=kOutput, calls=%fused_computation.28 | convolution fusion | flops 235929600 | bytes 2949120 | tf_op jit(solution)/shard_map/...c,cd->...d/dot_general | solution.py:28
  17.4 0.9 %fusion.17 = f32[2,2,8,36,320]{4,3,2,1,0:T(8,128)S(1)} fusion(bf16[2,2,10,36,320]{4,3,2,1,0:T(8,128)(2,1)S(1)} %fusion, bf16[3,3,320,320]{3,2,1,0:T(8,128)(2,1)S(1)} %copy-done.1), kind=kOutput, calls=%fused_computation.26 | convolution fusion | flops 235929600 | bytes 2949120 | tf_op jit(solution)/shard_map/...c,cd->...d/dot_general | solution.py:28
  18.2 0.9 %fusion.15 = f32[2,2,8,36,320]{4,3,2,1,0:T(8,128)S(1)} fusion(bf16[2,2,10,36,320]{4,3,2,1,0:T(8,128)(2,1)S(1)} %fusion, bf16[3,3,320,320]{3,2,1,0:T(8,128)(2,1)S(1)} %copy-done.1), kind=kOutput, calls=%fused_computation.24 | convolution fusion | flops 235929600 | bytes 2949120 | tf_op jit(solution)/shard_map/...c,cd->...d/dot_general | solution.py:28
  19.1 0.9 %fusion.13 = f32[2,2,8,36,320]{4,3,2,1,0:T(8,128)S(1)} fusion(bf16[2,2,10,36,320]{4,3,2,1,0:T(8,128)(2,1)S(1)} %fusion, bf16[3,3,320,320]{3,2,1,0:T(8,128)(2,1)S(1)} %copy-done.1), kind=kOutput, calls=%fused_computation.22 | convolution fusion | flops 235929600 | bytes 2949120 | tf_op jit(solution)/shard_map/...c,cd->...d/dot_general | solution.py:28
  20.0 0.8 %fusion.76 = f32[2,2,8,36,320]{4,3,2,1,0:T(8,128)S(1)} fusion(bf16[2,2,10,36,320]{4,3,2,1,0:T(8,128)(2,1)S(1)} %fusion, bf16[3,3,320,320]{3,2,1,0:T(8,128)(2,1)S(1)} %copy-done.1), kind=kOutput, calls=%fused_computation.89 | convolution fusion | flops 235929600 | bytes 2949120 | tf_op jit(solution)/shard_map/...c,cd->...d/dot_general | solution.py:28
  20.8 0.8 %fusion.80 = f32[2,2,8,36,320]{4,3,2,1,0:T(8,128)S(1)} fusion(bf16[2,2,10,36,320]{4,3,2,1,0:T(8,128)(2,1)S(1)} %fusion, bf16[3,3,320,320]{3,2,1,0:T(8,128)(2,1)S(1)} %copy-done.1), kind=kOutput, calls=%fused_computation.93 | convolution fusion | flops 235929600 | bytes 2949120 | tf_op jit(solution)/shard_map/...c,cd->...d/dot_general | solution.py:28
  21.7 0.9 %fusion.23 = f32[2,2,8,36,320]{4,3,2,1,0:T(8,128)S(1)} fusion(bf16[2,2,10,36,320]{4,3,2,1,0:T(8,128)(2,1)S(1)} %fusion, bf16[3,3,320,320]{3,2,1,0:T(8,128)(2,1)S(1)} %copy-done.1), kind=kOutput, calls=%fused_computation.32 | convolution fusion | flops 235929600 | bytes 2949120 | tf_op jit(solution)/shard_map/...c,cd->...d/dot_general | solution.py:28
  22.5 1.9 %add_convert_fusion = bf16[2,2,8,36,320]{4,3,2,1,0:T(8,128)(2,1)S(1)} fusion(f32[2,2,8,36,320]{4,3,2,1,0:T(8,128)S(1)} %fusion.13, f32[2,2,8,36,320]{4,3,2,1,0:T(8,128)S(1)} %fusion.15, f32[2,2,8,36,320]{4,3,2,1,0:T(8,128)S(1)} %fusion.17, f32[2,2,8,36,320]{4,3,2,1,0:T(8,128)S(1)} %fusion.76, f32[2,2,8,36,320]{4,3,2,1,0:T(8,128)S(1)} %fusion.19, ...), kind=kOutput, calls=%fused_computation.2 | convolution fusion | flops 239616000 | bytes 18923520 | tf_op jit(solution)/shard_map/...c,cd->...d/dot_general | solution.py:28
  24.5 1.4 %collective-permute-start.3 = (bf16[1,2,8,36,320]{4,3,2,0,1:T(8,128)(2,1)S(1)}, bf16[1,2,8,36,320]{4,3,2,0,1:T(8,128)(2,1)S(1)}, u32[]{:S(2)}, u32[]{:S(2)}) collective-permute-start(bf16[1,2,8,36,320]{4,3,2,0,1:T(8,128)(2,1)S(1)} %get-tuple-element.8), channel_id=1, source_target_pairs={{2,0},{4,2},{6,4},{8,6},{10,8},{12,10},{14,12},{16,14},{18,16},{20... | collective-permute-start | bytes 1105928 | tf_op jit(solution)/shard_map/ppermute | solution.py:15
  26.5 5.5 %collective-permute-start.2 = (bf16[1,2,8,36,320]{4,3,2,0,1:T(8,128)(2,1)S(1)}, bf16[1,2,8,36,320]{4,3,2,0,1:T(8,128)(2,1)S(1)}, u32[]{:S(2)}, u32[]{:S(2)}) collective-permute-start(bf16[1,2,8,36,320]{4,3,2,0,1:T(8,128)(2,1)S(1)} %get-tuple-element.7), channel_id=1, source_target_pairs={{0,2},{2,4},{4,6},{6,8},{8,10},{10,12},{12,14},{14,16},{16,18},{18... | collective-permute-start | bytes 1105928 | tf_op jit(solution)/shard_map/ppermute | solution.py:12
  32.6 9.1 %collective-permute-done.3 = bf16[1,2,8,36,320]{4,3,2,0,1:T(8,128)(2,1)S(1)} collective-permute-done((bf16[1,2,8,36,320]{4,3,2,0,1:T(8,128)(2,1)S(1)}, bf16[1,2,8,36,320]{4,3,2,0,1:T(8,128)(2,1)S(1)}, u32[]{:S(2)}, u32[]{:S(2)}) %collective-permute-start.3) | collective-permute-done | bytes 368672 | tf_op jit(solution)/shard_map/ppermute | solution.py:15
  42.7 10.3 %collective-permute-done.2 = bf16[1,2,8,36,320]{4,3,2,0,1:T(8,128)(2,1)S(1)} collective-permute-done((bf16[1,2,8,36,320]{4,3,2,0,1:T(8,128)(2,1)S(1)}, bf16[1,2,8,36,320]{4,3,2,0,1:T(8,128)(2,1)S(1)}, u32[]{:S(2)}, u32[]{:S(2)}) %collective-permute-start.2) | collective-permute-done | bytes 368672 | tf_op jit(solution)/shard_map/ppermute | solution.py:12
  53.5 1.0 %fusion.12 = bf16[2,8,36,320]{3,2,1,0:T(8,128)(2,1)S(1)} fusion(f32[2,8,36,320]{3,2,1,0:T(8,128)S(1)} %fusion.9, f32[2,8,36,320]{3,2,1,0:T(8,128)S(1)} %fusion.51, f32[2,8,36,320]{3,2,1,0:T(8,128)S(1)} %fusion.54, bf16[2,2,8,36,320]{4,3,2,0,1:T(8,128)(2,1)S(1)} %bitcast.200, bf16[1,2,8,36,320]{4,3,2,0,1:T(8,128)(2,1)S(1)} %collective-permute-done.2, ...), kind=kOutput, calls=%fused_computation.20 | convolution fusion | flops 121282560 | bytes 6021120 | tf_op jit(solution)/shard_map/...c,cd->...d/dot_general | solution.py:36
  54.5 0.8 %copy.13 = bf16[2,8,36,320]{3,1,2,0:T(8,128)(2,1)} copy(bf16[2,8,36,320]{3,2,1,0:T(8,128)(2,1)S(1)} %fusion.12) | data formatting | bytes 737280 | tf_op jit(solution)/shard_map/convert_element_type | solution.py:66
  (30 shorter events, 6.3 us)
Async XLA Ops:
  0.0 5.5 %copy-start = (bf16[2,8,36,320]{3,1,2,0:T(8,128)(2,1)S(1)}, bf16[2,8,36,320]{3,1,2,0:T(8,128)(2,1)}, u32[]{:S(2)}) copy-start(bf16[2,8,36,320]{3,1,2,0:T(8,128)(2,1)} %param.6) | copy-start | bytes 1105924
  1.2 5.4 %collective-permute-start.1 = (bf16[2,2,36,320]{3,2,1,0:T(8,128)(2,1)S(1)}, bf16[2,2,36,320]{3,2,1,0:T(8,128)(2,1)S(1)}, u32[]{:S(2)}, u32[]{:S(2)}) collective-permute-start(bf16[2,2,36,320]{3,2,1,0:T(8,128)(2,1)S(1)} %get-tuple-element.9), channel_id=1, source_target_pairs={{1,0},{3,2},{5,4},{7,6},{9,8},{11,10},{13,12},{15,14},{17,16},{19,... | collective-permute-start | bytes 276488 | tf_op jit(solution)/shard_map/ppermute | solution.py:15
  2.5 4.0 %collective-permute-start = (bf16[2,2,36,320]{3,2,1,0:T(8,128)(2,1)S(1)}, bf16[2,2,36,320]{3,2,1,0:T(8,128)(2,1)S(1)}, u32[]{:S(2)}, u32[]{:S(2)}) collective-permute-start(bf16[2,2,36,320]{3,2,1,0:T(8,128)(2,1)S(1)} %get-tuple-element.10), channel_id=1, source_target_pairs={{0,1},{2,3},{4,5},{6,7},{8,9},{10,11},{12,13},{14,15},{16,17},{18,... | collective-permute-start | bytes 276488 | tf_op jit(solution)/shard_map/ppermute | solution.py:12
  6.6 1.8 %copy-start.3 = (bf16[3,3,320,320]{3,2,1,0:T(8,128)(2,1)S(1)}, bf16[3,3,320,320]{3,2,1,0:T(8,128)(2,1)}, u32[]{:S(2)}) copy-start(bf16[3,3,320,320]{3,2,1,0:T(8,128)(2,1)} %param.7) | copy-start | bytes 5529604
  12.0 0.7 %copy-start.4 = (f32[320]{0:T(512)S(1)}, f32[320]{0:T(512)}, u32[]{:S(2)}) copy-start(f32[320]{0:T(512)} %param.10) | copy-start | bytes 3844
  12.0 0.7 %copy-start.5 = (f32[320]{0:T(512)S(1)}, f32[320]{0:T(512)}, u32[]{:S(2)}) copy-start(f32[320]{0:T(512)} %param.11) | copy-start | bytes 3844
  14.0 1.6 %copy-start.1 = (bf16[3,3,320,320]{3,2,1,0:T(8,128)(2,1)S(1)}, bf16[3,3,320,320]{3,2,1,0:T(8,128)(2,1)}, u32[]{:S(2)}) copy-start(bf16[3,3,320,320]{3,2,1,0:T(8,128)(2,1)} %param.8) | copy-start | bytes 5529604
  24.4 1.6 %copy-start.2 = (bf16[3,320,320]{2,1,0:T(8,128)(2,1)S(1)}, bf16[3,320,320]{2,1,0:T(8,128)(2,1)}, u32[]{:S(2)}) copy-start(bf16[3,320,320]{2,1,0:T(8,128)(2,1)} %param.9) | copy-start | bytes 1843204
  24.5 17.1 %collective-permute-start.3 = (bf16[1,2,8,36,320]{4,3,2,0,1:T(8,128)(2,1)S(1)}, bf16[1,2,8,36,320]{4,3,2,0,1:T(8,128)(2,1)S(1)}, u32[]{:S(2)}, u32[]{:S(2)}) collective-permute-start(bf16[1,2,8,36,320]{4,3,2,0,1:T(8,128)(2,1)S(1)} %get-tuple-element.8), channel_id=1, source_target_pairs={{2,0},{4,2},{6,4},{8,6},{10,8},{12,10},{14,12},{16,14},{18,16},{20... | collective-permute-start | bytes 1105928 | tf_op jit(solution)/shard_map/ppermute | solution.py:15
  26.5 26.5 %collective-permute-start.2 = (bf16[1,2,8,36,320]{4,3,2,0,1:T(8,128)(2,1)S(1)}, bf16[1,2,8,36,320]{4,3,2,0,1:T(8,128)(2,1)S(1)}, u32[]{:S(2)}, u32[]{:S(2)}) collective-permute-start(bf16[1,2,8,36,320]{4,3,2,0,1:T(8,128)(2,1)S(1)} %get-tuple-element.7), channel_id=1, source_target_pairs={{0,2},{2,4},{4,6},{6,8},{8,10},{10,12},{12,14},{14,16},{16,18},{18... | collective-permute-start | bytes 1105928 | tf_op jit(solution)/shard_map/ppermute | solution.py:12
where the time goes:
time: 55.6 us; the launch traced here: 55.3 us
  waiting for transfers between devices  20.2 us (36%)
  matrix products  19.4 us (35%)
  starting transfers between devices  11.3 us (20%)
  local copies, waits for them, and re-layouts  3.68 us (7%)
    dot_general x18, matrix products, spatial(): jnp.einsum('...c,cd->...d', window, weight[a, b], preferred_element_type=...  15.9 us
    ppermute x2, waiting for transfers between devices, with_halo(): lax.ppermute(lax.slice_in_dim(block, block.shape[dim] - width, None, axis...  11.1 us
    ppermute x2, waiting for transfers between devices, with_halo(): lax.ppermute(lax.slice_in_dim(block, 0, width, axis=dim), axis, backward)  9.07 us
    ppermute x2, starting transfers between devices, with_halo(): lax.ppermute(lax.slice_in_dim(block, block.shape[dim] - width, None, axis...  8.57 us
    ppermute x2, starting transfers between devices, with_halo(): lax.ppermute(lax.slice_in_dim(block, 0, width, axis=dim), axis, backward)  2.72 us
    unnamed x15, local copies, waits for them, and re-layouts  2.65 us
    dot_general x2, matrix products, temporal(): jnp.einsum('...c,cd->...d', padded[:-2], first_tap, preferred_element_typ...  1.48 us
  transfers between devices with their start and end apart: 4, of which 3 were waited for; matrix products, arithmetic and copies ran while one was open for 4% of the time, Pallas kernels for 0%

commit v1 on v0

v1 whole, which is shorter than its diff:
```python
import functools

import jax
import jax.numpy as jnp
from jax import lax
from jax.experimental import pallas as pl
from jax.experimental.pallas import tpu as pltpu
from jax.sharding import PartitionSpec as P

F32 = jnp.float32
BF16 = jnp.bfloat16
LANES = 128
SUB = 8
CHUNK = 2

NEAR, FAR, TAP_FAR, TAP_NEAR, HAS_FAR, HAS_UP, HAS_DOWN = range(7)


def silu(u):
    return 0.5 * u * (1.0 + jnp.tanh(0.5 * u))


def split(value, main):
    tail = value[..., main:]
    return value[..., :main], jnp.concatenate([tail, jnp.zeros_like(tail)], axis=-1)


def rows_of(shape):
    return lax.broadcasted_iota(jnp.int32, shape, len(shape) - 2)


def turn(value, shift):
    shift %= value.shape[-2]
    return value if shift == 0 else pltpu.roll(value, shift, value.ndim - 2)


def beside(low, high):
    return low + pltpu.roll(high, LANES // 2, high.ndim - 1)


def half_tile(value, which):
    lane = lax.broadcasted_iota(jnp.int32, value.shape, value.ndim - 1)
    if which:
        value = pltpu.roll(value, LANES // 2, value.ndim - 1)
    return jnp.where(lane < LANES // 2, value, 0.0)


def pack(low, high):
    (low_main, low_tail), (high_main, high_tail) = low, high
    return jnp.concatenate([low_main, high_main, beside(low_tail, high_tail)], axis=-1)


def unpack(value, main, which):
    return value[..., which * main : (which + 1) * main], half_tile(value[..., 2 * main :], which)


def edge_rows(first, second):
    row = rows_of(first.shape)
    return jnp.where(
        row < 2, first, jnp.where(row < 4, turn(first, 4), jnp.where(row < 6, turn(second, 4), second))
    )


class Stencil:
    def __init__(self, here, later, main):
        self.here, self.later, self.main = here, later, main
        self.held = None
        self.at = 0

    def add(self, prev, mid, nxt, first=None):
        pieces = [prev[0], mid[0], nxt[0], beside(prev[1], mid[1]), nxt[1]]
        if self.held is None:
            self.held = [jnp.zeros_like(p[:1]) for p in pieces] if first is None else first
        lane, start = 0, self.at * SUB
        for i, piece in enumerate(pieces):
            size, width = piece.shape[0] * SUB, piece.shape[-1]
            self.here[start : start + size, lane : lane + width] = piece.reshape(size, width).astype(BF16)
            moved = jnp.concatenate([self.held[i], piece[:-1]], axis=0)
            self.later[start : start + size, lane : lane + width] = moved.reshape(size, width).astype(BF16)
            self.held[i] = piece[-1:]
            lane += width
        self.at += pieces[0].shape[0]

    def close(self, last=None):
        lane, start = 0, self.at * SUB
        for i, held in enumerate(self.held):
            width = held.shape[-1]
            after = jnp.zeros_like(held) if last is None else last[i]
            moved = jnp.concatenate([held, after], axis=0)
            self.later[start : start + 2 * SUB, lane : lane + width] = moved.reshape(2 * SUB, width).astype(BF16)
            lane += width
        self.size = start

    def conv(self, weight):
        size, main = self.size, self.main

        def taps(column):
            parts = [weight[a, column, :main] for a in range(3)] + [weight[a, column, main:] for a in range(3)]
            return jnp.concatenate(parts + [jnp.zeros_like(parts[-1])], axis=0)

        total = jnp.dot(self.here[:size], taps(1), preferred_element_type=F32)
        total += jnp.dot(self.later[:size], taps(0), preferred_element_type=F32)
        total += jnp.dot(self.later[2 * SUB : 2 * SUB + size], taps(2), preferred_element_type=F32)
        return total


def columns(ref, start, main, size=CHUNK):
    return split(ref[start : start + size].astype(F32), main)


def conv_main(cols, main, source, weight, here, later):
    stencil = Stencil(here, later, main)
    for c in range(0, cols, CHUNK):
        mid = source(c)
        stencil.add([turn(p, 1) for p in mid], mid, [turn(p, -1) for p in mid])
    stencil.close()
    return stencil.conv(weight)


def edge_stencil(flags, own, up, down, main, here, later):
    stencil = Stencil(here, later, main)
    count = own.shape[0]

    def one(start, size):
        middle = columns(own, start, main, size)
        above = [jnp.where(flags[HAS_UP] > 0, p, 0.0) for p in columns(up, start, main, size)]
        below = [jnp.where(flags[HAS_DOWN] > 0, p, 0.0) for p in columns(down, start, main, size)]
        prev, mid, nxt = [], [], []
        for m, a, b in zip(middle, above, below):
            j = lax.rem(rows_of(m.shape), 4)
            prev.append(jnp.where(j < 2, turn(a, -2), m))
            mid.append(
                jnp.where(j < 1, turn(a, -3), jnp.where(j < 2, turn(m, 1), jnp.where(j < 3, turn(m, -1), turn(b, 3))))
            )
            nxt.append(jnp.where(j < 2, m, turn(b, 2)))
        return prev, mid, nxt

    return stencil, one, count


def edge_hidden(flags, total, cond, main):
    u = total + cond
    j = lax.rem(rows_of(u.shape), 4)
    h = silu(u)
    h = jnp.where((j > 0) | (flags[HAS_UP] > 0), h, 0.0)
    return jnp.where((j < 3) | (flags[HAS_DOWN] > 0), h, 0.0)


def second_conv(cols, main, spread, edges, cond, weight, here, later):
    stencil = Stencil(here, later, main)
    for c in range(0, cols, CHUNK):
        u = spread[c * SUB : (c + CHUNK) * SUB] + cond
        h = split(silu(u).reshape(CHUNK, SUB, u.shape[-1]), main)
        edge, base = edges(c)
        prev, mid, nxt = [], [], []
        for v, e in zip(h, edge):
            row = rows_of(v.shape)
            v = jnp.where(row == 0, turn(e, -(base + 1)), jnp.where(row == 7, turn(e, 7 - (base + 2)), v))
            mid.append(v)
            prev.append(jnp.where(row == 0, turn(e, -base), turn(v, 1)))
            nxt.append(jnp.where(row == 7, turn(e, 7 - (base + 3)), turn(v, -1)))
        stencil.add(prev, mid, nxt)
    stencil.close()
    return stencil.conv(weight)


def prepare_kernel(main, flags, video, edge, sent):
    cols = video.shape[1]
    near, far = flags[NEAR], flags[FAR]
    half = cols // 2
    for c in range(0, half, CHUNK):
        low = split(video[far, c : c + CHUNK].astype(F32), main)
        high = split(video[far, half + c : half + c + CHUNK].astype(F32), main)
        sent[c : c + CHUNK] = pack(low, high).astype(BF16)
    for c in range(0, cols, CHUNK):
        edge[c : c + CHUNK] = edge_rows(video[near, c : c + CHUNK].astype(F32), video[far, c : c + CHUNK].astype(F32)).astype(BF16)


def own_kernel(main, flags, video, weight, spread, here, later):
    cols = video.shape[1]
    for i, which in enumerate((NEAR, FAR)):
        f = flags[which]
        spread[i] = conv_main(
            cols, main, lambda c: split(video[f, c : c + CHUNK].astype(F32), main), weight, here.at[i], later.at[i]
        )


def residual(cols, main, source, spread, edges, conds, second, here, later, write):
    for p in range(2):
        added = second_conv(cols, main, spread, functools.partial(edges, p), conds[p], second, here.at[p], later.at[p])
        write(p, source, added)


def edge_kernel(main, flags, video, own, up, down, spread, cond, first, second, edge_h, r, sent, here, later):
    cols = video.shape[1]
    stencil, one, count = edge_stencil(flags, own, up, down, main, here.at[0], later.at[0])
    for c in range(0, count, CHUNK):
        stencil.add(*one(c, CHUNK))
    stencil.close()
    total = stencil.conv(first)
    total = total.reshape(count, SUB, total.shape[-1])
    for p in range(2):
        edge_h[p] = edge_hidden(flags, total, cond[p : p + 1], main)
    near = flags[NEAR]
    for p in range(2):
        added = second_conv(
            cols, main, spread.at[0], lambda c: (split(edge_h[p, c : c + CHUNK], main), 0), cond[p : p + 1], second,
            here.at[p], later.at[p],
        )
        r[p] = (video[near].astype(F32).reshape(added.shape) + added).astype(BF16)
    size = CHUNK * SUB
    for s in range(0, cols * SUB, size):
        low, high = (split(r[p, s : s + size].astype(F32), main) for p in range(2))
        sent[s : s + size] = pack(low, high).astype(BF16)


def relay_kernel(main, got, edge):
    half = got.shape[0]
    for c in range(0, half, CHUNK):
        value = got[c : c + CHUNK].astype(F32)
        low, high = unpack(value, main, 0), unpack(value, main, 1)
        tail = edge.shape[-1] - main
        edge[c : c + CHUNK, :, :main] = edge_rows(low[0], high[0]).astype(BF16)
        edge[c : c + CHUNK, :, main:] = edge_rows(low[1], high[1])[..., :tail].astype(BF16)


def other_kernel(main, flags, video, spread, edge_h, cond, second, got, first, r, far_spread, here, later):
    cols = video.shape[1]
    far = flags[FAR]
    for p in range(2):
        added = second_conv(
            cols, main, spread.at[1], lambda c: (split(edge_h[p, c : c + CHUNK], main), 4), cond[p : p + 1], second,
            here.at[p], later.at[p],
        )
        r[p] = (video[far].astype(F32).reshape(added.shape) + added).astype(BF16)
    half = cols // 2
    far_spread[...] = conv_main(
        cols, main, lambda c: unpack(got[c % half : c % half + CHUNK].astype(F32), main, c // half), first,
        here.at[0], later.at[0],
    )


def far_kernel(main, flags, got, own, up, down, spread, cond, first, second, r_near, r_far, taps, out, mixed, edge_h, r, here, later):
    half = got.shape[0]
    cols = 2 * half
    stencil, one, count = edge_stencil(flags, own, up, down, main, here.at[0], later.at[0])

    def pieces(column):
        prev, mid, nxt = one(column, 1)
        return [prev[0], mid[0], nxt[0], beside(prev[1], mid[1]), nxt[1]]

    before = [jnp.where(rows_of(p.shape) < 4, 0.0, turn(p, 4)) for p in pieces(count - 1)]
    after = [jnp.where(rows_of(p.shape) < 4, turn(p, 4), 0.0) for p in pieces(0)]
    for c in range(0, count, CHUNK):
        stencil.add(*one(c, CHUNK), first=before)
    stencil.close(after)
    total = stencil.conv(first)
    total = total.reshape(count, SUB, total.shape[-1])
    for p in range(2):
        edge_h[p] = edge_hidden(flags, total, cond[p : p + 1], main)
    size = CHUNK * SUB
    for p in range(2):
        added = second_conv(
            cols, main, spread, lambda c: (split(edge_h[p, c % half : c % half + CHUNK], main), c // half * 4),
            cond[p : p + 1], second, here.at[p], later.at[p],
        )
        for c in range(0, cols, CHUNK):
            x = unpack(got[c % half : c % half + CHUNK].astype(F32), main, c // half)
            s = c * SUB
            for x_part, at in zip(x, (slice(0, main), slice(main, added.shape[-1]))):
                part = added[s : s + size, at]
                x_part = x_part.reshape(size, x_part.shape[-1])[:, : part.shape[-1]]
                r[p, s : s + size, at] = jnp.where(flags[HAS_FAR] > 0, x_part + part, 0.0).astype(BF16)
    to_far, to_near = taps[flags[TAP_FAR]], taps[flags[TAP_NEAR]]
    blend = None
    for p in range(2):
        earlier, later_tap = (to_far, to_near) if p == 0 else (to_near, to_far)
        t = jnp.dot(r[p], earlier, preferred_element_type=F32)
        t += jnp.dot(r_far[p], taps[1], preferred_element_type=F32)
        t += jnp.dot(r_near[p], later_tap, preferred_element_type=F32)
        t = r_far[p].astype(F32) + silu(t)
        blend = t if blend is None else blend + t
        mixed[p] = jnp.dot(r_far[p], earlier, preferred_element_type=F32) + jnp.dot(
            r_near[p], taps[1], preferred_element_type=F32
        )
    out[...] = (0.5 * blend).astype(BF16)


def last_kernel(main, flags, got, mixed, r_near, taps, done, out, staged, sems):
    tail = r_near.shape[-1] - main
    first = pltpu.make_async_copy(done, out.at[flags[FAR]], sems.at[0])
    first.start()
    to_far, to_near = taps[flags[TAP_FAR]], taps[flags[TAP_NEAR]]
    blend = None
    for p in range(2):
        tap = to_near if p == 0 else to_far
        tail_value = half_tile(got[:, 2 * main :].astype(F32), p).astype(BF16)
        t = mixed[p] + jnp.dot(got[:, p * main : (p + 1) * main], tap[:main], preferred_element_type=F32)
        t += jnp.dot(tail_value[:, :tail], tap[main:], preferred_element_type=F32)
        t = r_near[p].astype(F32) + silu(t)
        blend = t if blend is None else blend + t
    staged[...] = (0.5 * blend).astype(BF16).reshape(staged.shape)
    second = pltpu.make_async_copy(staged, out.at[flags[NEAR]], sems.at[1])
    second.start()
    first.wait()
    second.wait()


VMEM = pl.BlockSpec(memory_space=pltpu.VMEM)
SMEM = pl.BlockSpec(memory_space=pltpu.SMEM)
ANY = pl.BlockSpec(memory_space=pl.ANY)


def call(kernel, outs, args, scratch=(), name=None, flops=0, out_specs=None, limit=20):
    return pl.pallas_call(
        kernel,
        out_shape=outs,
        in_specs=[SMEM if a.dtype == jnp.int32 else VMEM for a in args],
        out_specs=out_specs or jax.tree.map(lambda _: VMEM, outs),
        scratch_shapes=list(scratch),
        name=name,
        cost_estimate=pl.CostEstimate(flops=flops, bytes_accessed=1 << 20, transcendentals=0),
        compiler_params=pltpu.CompilerParams(vmem_limit_bytes=limit << 20),
    )(*args)


def pairs(count, start):
    links = [(i, i + 1) for i in range(start, count - 1, 2)]
    return links + [(b, a) for a, b in links]


def row_neighbours(edge):
    count = lax.axis_size("row")
    if count == 1:
        return edge, edge
    first = lax.ppermute(edge, "row", pairs(count, 0))
    if count == 2:
        return first, first
    second = lax.ppermute(edge, "row", pairs(count, 1))
    even = lax.axis_index("row") % 2 == 0
    return jnp.where(even, second, first), jnp.where(even, first, second)


def shards(latents, conv_first, conv_second, conv_time, cond_start, cond_end):
    _, rows, cols, channels = latents.shape
    main = channels // LANES * LANES
    assert latents.shape[0] == 2 and rows == SUB and 2 * (channels - main) == LANES and cols % (2 * CHUNK) == 0
    pixels = rows * cols
    width = 3 * main + 2 * LANES
    frames_n, rows_n = lax.axis_size("frame"), lax.axis_size("row")
    frame, row = lax.axis_index("frame"), lax.axis_index("row")
    odd = frame % 2
    has_far = jnp.where(odd == 1, frame < frames_n - 1, frame > 0)
    flags = jnp.stack([1 - odd, odd, 2 * odd, 2 - 2 * odd, has_far, row > 0, row < rows_n - 1]).astype(jnp.int32)

    video = jnp.transpose(latents, (0, 2, 1, 3))
    cond = jnp.stack([cond_start, cond_end])
    taps = channels * channels * 2

    def struct(*shape, dtype=BF16):
        return jax.ShapeDtypeStruct(shape, dtype)

    stencils = [pltpu.VMEM((2, pixels, width), BF16), pltpu.VMEM((2, pixels + 2 * SUB, width), BF16)]
    edge, sent = call(
        functools.partial(prepare_kernel, main),
        (struct(cols, SUB, channels), struct(cols // 2, SUB, 2 * main + LANES)),
        (flags, video), name="prepare",
    )
    got_far = lax.ppermute(sent, "frame", pairs(frames_n, 1))
    up, down = row_neighbours(edge)
    spread = call(
        functools.partial(own_kernel, main), struct(2, pixels, channels, dtype=F32), (flags, video, conv_first),
        stencils, "own", 18 * pixels * taps,
    )
    edge_h, r_near, sent_near = call(
        functools.partial(edge_kernel, main),
        (struct(2, cols, SUB, channels, dtype=F32), struct(2, pixels, channels), struct(pixels, 2 * main + LANES)),
        (flags, video, edge, up, down, spread, cond, conv_first, conv_second), stencils, "near", 27 * pixels * taps,
    )
    got_near = lax.ppermute(sent_near, "frame", pairs(frames_n, 0))
    far_edge = call(functools.partial(relay_kernel, main), struct(cols // 2, SUB, channels), (got_far,), name="relay")
    far_up, far_down = row_neighbours(far_edge)
    r_far, far_spread = call(
        functools.partial(other_kernel, main), (struct(2, pixels, channels), struct(pixels, channels, dtype=F32)),
        (flags, video, spread, edge_h, cond, conv_second, got_far, conv_first), stencils, "other", 27 * pixels * taps,
    )
    done, mixed = call(
        functools.partial(far_kernel, main), (struct(pixels, channels), struct(2, pixels, channels, dtype=F32)),
        (flags, got_far, far_edge, far_up, far_down, far_spread, cond, conv_first, conv_second, r_near, r_far, conv_time),
        [pltpu.VMEM((2, cols // 2, SUB, channels), F32), pltpu.VMEM((2, pixels, channels), BF16), *stencils],
        "far", 33 * pixels * taps,
    )
    out = call(
        functools.partial(last_kernel, main), struct(2, cols, SUB, channels),
        (flags, got_near, mixed, r_near, conv_time, done.reshape(cols, SUB, channels)),
        [pltpu.VMEM((cols, SUB, channels), BF16), pltpu.SemaphoreType.DMA((2,))], "last", 2 * pixels * taps, ANY,
    )
    return jnp.transpose(out, (0, 2, 1, 3))


def solution(mesh):
    placed = (P("frame", "row", None, None), P(), P(), P(), P(), P())
    return jax.shard_map(
        shards, mesh=mesh, in_specs=placed, out_specs=P("frame", "row", None, None), check_vma=False
    )
```

time: 55.6 us -> 31.4 us (0.56)
  waiting for transfers between devices: 20.2 us -> 0.01 us
  matrix products: 19.4 us -> 0 us
  Pallas kernels: 0 us -> 18.7 us
  starting transfers between devices: 11.3 us -> 6.58 us
  local copies, waits for them, and re-layouts: 3.68 us -> 5.73 us
    ppermute x4, waiting for transfers between devices: 20.2 us -> 0.01 us  [the longest x2 0.01 us: row_neighbours(): first = lax.ppermute(edge, 'row', pairs(count, 0))]
    dot_general x24 -> x0, matrix products: 19.4 us -> none  [the longest x18 15.9 us: spatial(): jnp.einsum('...c,cd->...d', window, weight[a, b], preferred_element_type=...]
    pallas_call x0 -> x7, Pallas kernels: none -> 18.7 us  [call(): pl.pallas_call(kernel, out_shape=outs, in_specs=[SMEM if a.dtype == jnp.i...]
    ppermute x4, starting transfers between devices: 11.3 us -> 6.58 us  [the longest x1 5.29 us: shards(): got_near = lax.ppermute(sent_near, 'frame', pairs(frames_n, 0))]
    unnamed x15 -> x14, local copies, waits for them, and re-layouts: 2.65 us -> 4.27 us
    another operation x0 -> x3, local copies, waits for them, and re-layouts: none -> 1.45 us  [the longest x2 1.37 us: shards(): cond = jnp.stack([cond_start, cond_end])]
    convert_element_type x2 -> x0, local copies, waits for them, and re-layouts: 0.88 us -> none  [the longest x1 0.82 us: shards(): return (0.5 * (forward + returned)).astype(jnp.bfloat16)]
  transfers between devices with their start and end apart: 4 -> 4, of which waited for: 3 -> 0; matrix products, arithmetic and copies ran while one was open for 4% -> 4% of each run, Pallas kernels for 0% -> 52%
where the time goes in v1:
time: 31.4 us; the launch traced here: 31.2 us
  Pallas kernels  18.7 us (60%)
  starting transfers between devices  6.58 us (21%)
  local copies, waits for them, and re-layouts  5.73 us (18%)
    pallas_call x7, Pallas kernels, call(): pl.pallas_call(kernel, out_shape=outs, in_specs=[SMEM if a.dtype == jnp.i...  18.7 us
    ppermute x1, starting transfers between devices, shards(): got_near = lax.ppermute(sent_near, 'frame', pairs(frames_n, 0))  5.29 us
    unnamed x14, local copies, waits for them, and re-layouts  4.27 us
    another operation x2, local copies, waits for them, and re-layouts, shards(): cond = jnp.stack([cond_start, cond_end])  1.37 us
    ppermute x1, starting transfers between devices, shards(): got_far = lax.ppermute(sent, 'frame', pairs(frames_n, 1))  0.66 us
    ppermute x2, starting transfers between devices, row_neighbours(): first = lax.ppermute(edge, 'row', pairs(count, 0))  0.63 us
  transfers between devices with their start and end apart: 4, of which 0 were waited for; matrix products, arithmetic and copies ran while one was open for 4% of the time, Pallas kernels for 52%

profile of v1, /device:TPU:0, one launch (start us, length us, event | category | flops | bytes accessed | tf_op | source)
XLA Modules:
  0.0 31.2 jit_solution(8820484340699387681)
XLA Ops:
  0.0 0.1 stack.52.flags
  0.1 1.0 %copy-done.4 = bf16[2,8,36,320]{3,1,2,0:T(8,128)(2,1)S(1)} copy-done((bf16[2,8,36,320]{3,1,2,0:T(8,128)(2,1)S(1)}, bf16[2,8,36,320]{3,1,2,0:T(8,128)(2,1)}, u32[]{:S(2)}) %copy-start.4) | copy-done | bytes 368664
  1.1 0.7 %prepare.1 = (bf16[36,8,320]{2,1,0:T(8,128)(2,1)S(1)}, bf16[18,8,640]{2,1,0:T(8,128)(2,1)S(1)}) custom-call(s32[7]{0:T(128)S(1)} %stack.52.flags, bf16[2,36,8,320]{3,2,1,0:T(8,128)(2,1)S(1)} %bitcast.10), custom_call_target="tpu_custom_call" | custom-call | bytes 1048576 | tf_op jit(solution)/shard_map/prepare/pallas_call | solution.py:315
  1.8 0.6 %collective-permute-start = (bf16[36,8,320]{2,1,0:T(8,128)(2,1)S(1)}, bf16[36,8,320]{2,1,0:T(8,128)(2,1)S(1)}, u32[]{:S(2)}, u32[]{:S(2)}) collective-permute-start(bf16[36,8,320]{2,1,0:T(8,128)(2,1)S(1)} %get-tuple-element.14.own), channel_id=1, source_target_pairs={{0,1},{1,0},{2,3},{3,2},{4,5},{5,4},{6,7},{7,6},{8,9},{9,8},{10,11... | collective-permute-start | bytes 552968 | tf_op jit(solution)/shard_map/ppermute | solution.py:336
  2.3 0.7 %collective-permute-start.2 = (bf16[18,8,640]{2,1,0:T(8,128)(2,1)S(1)}, bf16[18,8,640]{2,1,0:T(8,128)(2,1)S(1)}, u32[]{:S(2)}, u32[]{:S(2)}) collective-permute-start(bf16[18,8,640]{2,1,0:T(8,128)(2,1)S(1)} %get-tuple-element.16), channel_id=1, source_target_pairs={{2,4},{6,8},{10,12},{14,16},{18,20},{22,24},{26,28},{4,2},{8,6},{1... | collective-permute-start | bytes 552968 | tf_op jit(solution)/shard_map/ppermute | solution.py:369
  3.0 0.7 %stack.53 = f32[1,320]{1,0:T(1,128)S(1)} reshape(f32[320]{0:T(512)} %param.10) | data formatting | bytes 2560 | tf_op jit(solution)/shard_map/stack | solution.py:357
  3.7 0.7 %stack.54 = f32[1,320]{1,0:T(1,128)S(1)} reshape(f32[320]{0:T(512)} %param.11) | data formatting | bytes 2560 | tf_op jit(solution)/shard_map/stack | solution.py:357
  4.4 1.6 %copy-done = bf16[3,3,320,320]{3,2,1,0:T(8,128)(2,1)S(1)} copy-done((bf16[3,3,320,320]{3,2,1,0:T(8,128)(2,1)S(1)}, bf16[3,3,320,320]{3,2,1,0:T(8,128)(2,1)}, u32[]{:S(2)}) %copy-start) | copy-done | bytes 1843224
  6.0 2.6 %own.1.spread = f32[2,288,320]{2,1,0:T(8,128)S(1)} custom-call(s32[7]{0:T(128)S(1)} %stack.52.flags, bf16[2,36,8,320]{3,2,1,0:T(8,128)(2,1)S(1)} %bitcast.11, bf16[3,3,320,320]{3,2,1,0:T(8,128)(2,1)S(1)} %copy-done), custom_call_target="tpu_custom_call" | custom-call | flops 1061683200 | bytes 1048576 | tf_op jit(solution)/shard_map/own/pallas_call | solution.py:315
  8.6 0.0 collective-permute-done.up.down
  8.6 0.0 copy-done.1
  8.6 0.0 copy-start.2
  8.6 1.6 %copy-done.2 = bf16[3,3,320,320]{3,2,1,0:T(8,128)(2,1)S(1)} copy-done((bf16[3,3,320,320]{3,2,1,0:T(8,128)(2,1)S(1)}, bf16[3,3,320,320]{3,2,1,0:T(8,128)(2,1)}, u32[]{:S(2)}) %copy-start.2) | copy-done | bytes 1843224
  10.3 4.5 %near.1 = (f32[2,36,8,320]{3,2,1,0:T(8,128)S(1)}, bf16[2,288,320]{2,1,0:T(8,128)(2,1)S(1)}, bf16[288,640]{1,0:T(8,128)(2,1)S(1)}) custom-call(s32[7]{0:T(128)S(1)} %stack.52.flags, bf16[2,36,8,320]{3,2,1,0:T(8,128)(2,1)S(1)} %bitcast.12, bf16[36,8,320]{2,1,0:T(8,128)(2,1)S(1)} %get-tuple-element.14.own, ...), custom_call_target="tpu_custom_call" | custom-call | flops 1592524800 | bytes 1048576 | tf_op jit(solution)/shard_map/near/pallas_call | solution.py:315
  14.7 5.3 %collective-permute-start.1 = (bf16[288,640]{1,0:T(8,128)(2,1)S(1)}, bf16[288,640]{1,0:T(8,128)(2,1)S(1)}, u32[]{:S(2)}, u32[]{:S(2)}) collective-permute-start(bf16[288,640]{1,0:T(8,128)(2,1)S(1)} %get-tuple-element.15), channel_id=1, source_target_pairs={{0,2},{4,6},{8,10},{12,14},{16,18},{20,22},{24,26},{28,30},{2,0},{... | collective-permute-start | bytes 1105928 | tf_op jit(solution)/shard_map/ppermute | solution.py:380
  20.0 0.0 collective-permute-done.2.got
  20.0 0.1 relay.1.own
  20.1 0.1 collective-permute-start.3
  20.2 0.0 copy-start.6
  20.2 3.8 %other.1 = (bf16[2,288,320]{2,1,0:T(8,128)(2,1)S(1)}, f32[288,320]{1,0:T(8,128)S(1)}) custom-call(s32[7]{0:T(128)S(1)} %stack.52.flags, bf16[2,36,8,320]{3,2,1,0:T(8,128)(2,1)S(1)} %bitcast.13, f32[2,288,320]{2,1,0:T(8,128)S(1)} %own.1.spread, f32[2,36,8,320]{3,2,1,0:T(8,128)S(1)} %get-tuple-element.17.edge_h, f32[2,320]{1,0:T(2,128)S(1)} %pad_maximum_fusion.cond, ...), custom_call_target="tpu_custom_call" | custom-call | flops 1592524800 | bytes 1048576 | tf_op jit(solution)/shard_map/other/pallas_call | solution.py:315
  24.0 0.0 collective-permute-done.3.up.down
  24.1 5.3 %far.1 = (bf16[288,320]{1,0:T(8,128)(2,1)S(1)}, f32[2,288,320]{2,1,0:T(8,128)S(1)}) custom-call(s32[7]{0:T(128)S(1)} %stack.52.flags, bf16[18,8,640]{2,1,0:T(8,128)(2,1)S(1)} %collective-permute-done.2.got, bf16[18,8,320]{2,1,0:T(8,128)(2,1)S(1)} %relay.1.own, bf16[18,8,320]{2,1,0:T(8,128)(2,1)S(1)} %collective-permute-done.3.up.down, ...), custom_call_target="tpu_custom_call" | custom-call | flops 1946419200 | bytes 1048576 | tf_op jit(solution)/shard_map/far/pallas_call | solution.py:315
  29.4 0.0 collective-permute-done.1.got
  29.4 1.8 %last.1 = bf16[2,36,8,320]{3,2,1,0:T(8,128)(2,1)} custom-call(s32[7]{0:T(128)S(1)} %stack.52.flags, bf16[288,640]{1,0:T(8,128)(2,1)S(1)} %collective-permute-done.1.got, f32[2,288,320]{2,1,0:T(8,128)S(1)} %get-tuple-element.21.mixed, bf16[2,288,320]{2,1,0:T(8,128)(2,1)S(1)} %get-tuple-element.19.r_near, bf16[3,320,320]{2,1,0:T(8,128)(2,1)S(1)} %copy-done.6, ...), custom_call_target="tpu_custom_call" | custom-call | flops 117964800 | bytes 1048576 | tf_op jit(solution)/shard_map/last/pallas_call | solution.py:315
  (9 shorter events, 0.0 us)
Async XLA Ops:
  0.1 1.0 %copy-start.4 = (bf16[2,8,36,320]{3,1,2,0:T(8,128)(2,1)S(1)}, bf16[2,8,36,320]{3,1,2,0:T(8,128)(2,1)}, u32[]{:S(2)}) copy-start(bf16[2,8,36,320]{3,1,2,0:T(8,128)(2,1)} %param.6) | copy-start | bytes 1105924
  1.8 6.8 %collective-permute-start = (bf16[36,8,320]{2,1,0:T(8,128)(2,1)S(1)}, bf16[36,8,320]{2,1,0:T(8,128)(2,1)S(1)}, u32[]{:S(2)}, u32[]{:S(2)}) collective-permute-start(bf16[36,8,320]{2,1,0:T(8,128)(2,1)S(1)} %get-tuple-element.14.own), channel_id=1, source_target_pairs={{0,1},{1,0},{2,3},{3,2},{4,5},{5,4},{6,7},{7,6},{8,9},{9,8},{10,11... | collective-permute-start | bytes 552968 | tf_op jit(solution)/shard_map/ppermute | solution.py:336
  2.3 17.7 %collective-permute-start.2 = (bf16[18,8,640]{2,1,0:T(8,128)(2,1)S(1)}, bf16[18,8,640]{2,1,0:T(8,128)(2,1)S(1)}, u32[]{:S(2)}, u32[]{:S(2)}) collective-permute-start(bf16[18,8,640]{2,1,0:T(8,128)(2,1)S(1)} %get-tuple-element.16), channel_id=1, source_target_pairs={{2,4},{6,8},{10,12},{14,16},{18,20},{22,24},{26,28},{4,2},{8,6},{1... | collective-permute-start | bytes 552968 | tf_op jit(solution)/shard_map/ppermute | solution.py:369
  4.4 1.6 %copy-start = (bf16[3,3,320,320]{3,2,1,0:T(8,128)(2,1)S(1)}, bf16[3,3,320,320]{3,2,1,0:T(8,128)(2,1)}, u32[]{:S(2)}) copy-start(bf16[3,3,320,320]{3,2,1,0:T(8,128)(2,1)} %first.5) | copy-start | bytes 5529604
  6.0 2.6 %copy-start.1 = (bf16[3,3,320,320]{3,2,1,0:T(8,128)(2,1)S(1)}, bf16[3,3,320,320]{3,2,1,0:T(8,128)(2,1)}, u32[]{:S(2)}) copy-start(bf16[3,3,320,320]{3,2,1,0:T(8,128)(2,1)} %first.5) | copy-start | bytes 5529604
  8.6 1.6 %copy-start.2 = (bf16[3,3,320,320]{3,2,1,0:T(8,128)(2,1)S(1)}, bf16[3,3,320,320]{3,2,1,0:T(8,128)(2,1)}, u32[]{:S(2)}) copy-start(bf16[3,3,320,320]{3,2,1,0:T(8,128)(2,1)} %second.5) | copy-start | bytes 5529604
  10.3 9.9 %copy-start.3 = (bf16[3,3,320,320]{3,2,1,0:T(8,128)(2,1)S(1)}, bf16[3,3,320,320]{3,2,1,0:T(8,128)(2,1)}, u32[]{:S(2)}) copy-start(bf16[3,3,320,320]{3,2,1,0:T(8,128)(2,1)} %second.5) | copy-start | bytes 5529604
  10.3 9.9 %copy-start.5 = (bf16[2,8,36,320]{3,1,2,0:T(8,128)(2,1)S(1)}, bf16[2,8,36,320]{3,1,2,0:T(8,128)(2,1)}, u32[]{:S(2)}) copy-start(bf16[2,8,36,320]{3,1,2,0:T(8,128)(2,1)} %param.6) | copy-start | bytes 1105924
  14.7 14.6 %collective-permute-start.1 = (bf16[288,640]{1,0:T(8,128)(2,1)S(1)}, bf16[288,640]{1,0:T(8,128)(2,1)S(1)}, u32[]{:S(2)}, u32[]{:S(2)}) collective-permute-start(bf16[288,640]{1,0:T(8,128)(2,1)S(1)} %get-tuple-element.15), channel_id=1, source_target_pairs={{0,2},{4,6},{8,10},{12,14},{16,18},{20,22},{24,26},{28,30},{2,0},{... | collective-permute-start | bytes 1105928 | tf_op jit(solution)/shard_map/ppermute | solution.py:380
  20.1 3.9 %collective-permute-start.3 = (bf16[18,8,320]{2,1,0:T(8,128)(2,1)S(1)}, bf16[18,8,320]{2,1,0:T(8,128)(2,1)S(1)}, u32[]{:S(2)}, u32[]{:S(2)}) collective-permute-start(bf16[18,8,320]{2,1,0:T(8,128)(2,1)S(1)} %relay.1.own), channel_id=1, source_target_pairs={{0,1},{1,0},{2,3},{3,2},{4,5},{5,4},{6,7},{7,6},{8,9},{9,8},{10,11... | collective-permute-start | bytes 276488 | tf_op jit(solution)/shard_map/ppermute | solution.py:336
  20.2 3.8 %copy-start.6 = (bf16[3,320,320]{2,1,0:T(8,128)(2,1)S(1)}, bf16[3,320,320]{2,1,0:T(8,128)(2,1)}, u32[]{:S(2)}) copy-start(bf16[3,320,320]{2,1,0:T(8,128)(2,1)} %taps.3) | copy-start | bytes 1843204

commit v2 on v0

v2 whole, which is shorter than its diff:
```python
import functools

import jax
import jax.numpy as jnp
from jax import lax
from jax.experimental import pallas as pl
from jax.experimental.pallas import tpu as pltpu
from jax.sharding import PartitionSpec as P

F32 = jnp.float32
BF16 = jnp.bfloat16
LANES = 128
HALF = LANES // 2
SUB = 8
CHUNK = 2
PAD = 2 * SUB

NEAR, FAR, TAP_FAR, TAP_NEAR, HAS_FAR, HAS_UP, HAS_DOWN = range(7)


def split(value, main):
    tail = value[..., main:]
    if tail.shape[-1] < LANES:
        tail = jnp.concatenate([tail, jnp.zeros_like(tail)], axis=-1)
    return [value[..., :main], tail]


def rows_of(value):
    return lax.broadcasted_iota(jnp.int32, value.shape, value.ndim - 2)


def lanes_of(value):
    return lax.broadcasted_iota(jnp.int32, value.shape, value.ndim - 1)


def turn(value, shift):
    shift %= value.shape[-2]
    return value if shift == 0 else pltpu.roll(value, shift, value.ndim - 2)


def swap_halves(value):
    return pltpu.roll(value, HALF, value.ndim - 1)


def beside(low, high):
    return jnp.where(lanes_of(low) < HALF, low, swap_halves(high))


def unpack(value, main, which):
    tail = value[..., 2 * main :]
    return [value[..., which * main : (which + 1) * main], swap_halves(tail) if which else tail]


def store(ref, start, value):
    main, tail = value
    width = main.shape[-1]
    ref[pl.ds(start, main.shape[0]), :, :width] = main.astype(ref.dtype)
    ref[pl.ds(start, main.shape[0]), :, width:] = tail[..., : ref.shape[-1] - width].astype(ref.dtype)


def edges_of(column, count):
    def tile(g):
        outer, second = None, None
        for j in range(4):
            x = column(j * count + g)
            z = [jnp.where(rows_of(v) == 7, turn(v, 1), turn(v, -1)) for v in x]
            x, z = [turn(v, 2 * j) for v in x], [turn(v, 2 * j) for v in z]
            if j == 0:
                outer, second = x, z
            else:
                at = lambda v: (rows_of(v) == (2 * j + 7) % 8) | (rows_of(v) == 2 * j)
                outer = [jnp.where(at(v), v, o) for v, o in zip(x, outer)]
                second = [jnp.where(at(v), v, o) for v, o in zip(z, second)]
        return outer, second

    return tile


class Stencil:
    def __init__(self, here, start=0):
        self.here = here
        self.row = start

    @staticmethod
    def pieces(prev, mid, nxt):
        return [prev[0], mid[0], nxt[0], beside(prev[1], mid[1]), nxt[1]]

    def put(self, pieces):
        size, lane = pieces[0].shape[0] * SUB, 0
        for piece in pieces:
            width = piece.shape[-1]
            self.here[self.row : self.row + size, lane : lane + width] = piece.reshape(size, width).astype(BF16)
            lane += width
        self.row += size


def pack_tails(weight, tails, main):
    row = 0
    for part in (slice(0, main), slice(main, None)):
        for a in range(3):
            left, mid, right = (weight[a, b, part, main:] for b in range(3))
            size = left.shape[0]
            tails[row : row + size, :LANES] = jnp.concatenate([left, mid], axis=1)
            tails[row : row + size, LANES:] = jnp.concatenate([right, jnp.zeros_like(right)], axis=1)
            row += size
    tails[row:] = jnp.zeros_like(tails[row:])


def convolve(here, weight, tails, total, start, size, main, into=0):
    def taps(column):
        parts = [weight[a, column, :main, :main] for a in range(3)] + [weight[a, column, main:, :main] for a in range(3)]
        return jnp.concatenate(parts + [jnp.zeros_like(parts[-1])], axis=0)

    def left(by):
        first = start + by * SUB
        return here[first : first + size]

    rows = slice(into, into + size)
    out = jnp.dot(left(1), taps(1), preferred_element_type=F32)
    out += jnp.dot(left(0), taps(0), preferred_element_type=F32)
    out += jnp.dot(left(2), taps(2), preferred_element_type=F32)
    total[rows, :main] = out
    total[rows, main:] = jnp.dot(left(1), tails[...], preferred_element_type=F32)


def tail_of(left, mid, right):
    return left[..., :LANES] + swap_halves(mid[..., :LANES]) + right[..., LANES:]


def frame_sum(total, c, cols, main, base=0):
    out, tail = [], []
    for i in range(c, c + CHUNK):
        s = base + i * SUB
        mid = total[s : s + SUB, main:]
        left = total[s - SUB : s, main:] if i > 0 else jnp.zeros_like(mid)
        right = total[s + SUB : s + 2 * SUB, main:] if i < cols - 1 else jnp.zeros_like(mid)
        out.append(total[s : s + SUB, :main])
        tail.append(tail_of(left, mid, right))
    return [jnp.stack(out), jnp.stack(tail)]


def edge_sum(total, g, count, main, base):
    mid = total[base + g * SUB : base + (g + 1) * SUB, main:]
    row = rows_of(mid)
    if g > 0:
        left = total[base + (g - 1) * SUB : base + g * SUB, main:]
    else:
        left = jnp.where((row == 7) | (row == 0), 0.0, turn(total[base + (count - 1) * SUB : base + count * SUB, main:], 2))
    if g < count - 1:
        right = total[base + (g + 1) * SUB : base + (g + 2) * SUB, main:]
    else:
        right = jnp.where((row == 5) | (row == 6), 0.0, turn(total[base : base + SUB, main:], -2))
    return [total[base + g * SUB : base + (g + 1) * SUB, :main], tail_of(left, mid, right)]


def edge_stencil(flags, outer, up, down, count, main, here, start):
    nearby = []
    has_up, has_down = flags[HAS_UP] > 0, flags[HAS_DOWN] > 0

    def pieces(g):
        prev, mid, nxt = [], [], []
        ups, downs = [up(k, g) for k in range(2)], [down(k, g) for k in range(2)]
        own = outer(g)
        for i in range(2):
            above = lax.rem(rows_of(own[i]), 2) == 1
            crossed = jnp.where(above, turn(own[i], -1), turn(own[i], 1))
            u_out, u_sec = (jnp.where(has_up, ups[k][i], 0.0) for k in range(2))
            d_out, d_sec = (jnp.where(has_down, downs[k][i], 0.0) for k in range(2))
            prev.append(jnp.where(above, u_sec, crossed))
            mid.append(jnp.where(above, u_out, d_out))
            nxt.append(jnp.where(above, crossed, d_sec))
        nearby.append(mid)
        return [p[None] for p in Stencil.pieces(prev, mid, nxt)]

    def wrap(values, shift, first, last):
        return [jnp.where((rows_of(v) == first) | (rows_of(v) == last), 0.0, turn(v, shift)) for v in values]

    tiles = [pieces(g) for g in range(count)]
    before, after = wrap(tiles[-1], 2, 7, 0), wrap(tiles[0], -2, 5, 6)
    tiles = [before, *tiles, after]
    stencil = Stencil(here, start)
    for tile in tiles:
        stencil.put(tile)
    return nearby


def inner_stencil(column, edge, cols, count, here, start=0):
    stencil = Stencil(here, start)
    blank = None
    for c in range(0, cols, CHUNK):
        mid = column(c)
        outer = [[turn(v, -2 * (i // count)) for v in edge(i % count)] for i in range(c, c + CHUNK)]
        prev, nxt = [], []
        for k, v in enumerate(mid):
            e = jnp.stack([o[k] for o in outer])
            prev.append(turn(jnp.where(rows_of(v) == 7, e, v), 1))
            nxt.append(turn(jnp.where(rows_of(v) == 0, e, v), -1))
        pieces = Stencil.pieces(prev, mid, nxt)
        if blank is None:
            blank = [jnp.zeros_like(p[:1]) for p in pieces]
            stencil.put(blank)
        stencil.put(pieces)
    stencil.put(blank)


def half_silu(y):
    return y + y * jnp.tanh(y)


def stage(flags):
    return pl.when(flags[NEAR] >= 0)


def cond_halves(cond, main):
    return [0.5 * v for v in split(cond[...].reshape(1, cond.shape[-1]), main)]


def spread_halves(total, spread, cols, count, main, base, edge_base):
    for c in range(0, cols, CHUNK):
        store(spread, c, [0.5 * v for v in frame_sum(total, c, cols, main, base)])
    for g in range(count):
        store(spread, cols + g, [0.5 * v[None] for v in edge_sum(total, g, count, main, edge_base)])


def hidden_stencil(flags, spread, cond, cols, count, main, edge_h, here, start):
    halves = cond_halves(cond, main)
    for g in range(count):
        h = [half_silu(v + b) for v, b in zip(split_wide(spread, cols + g, 1, main), halves)]
        above = [lax.rem(rows_of(v), 2) == 1 for v in h]
        h = [
            jnp.where(jnp.where(a, flags[HAS_UP], flags[HAS_DOWN]) > 0, v, 0.0) for v, a in zip(h, above)
        ]
        store(edge_h, g, h)

    def column(c):
        return [half_silu(v + b) for v, b in zip(split_wide(spread, c, CHUNK, main), halves)]

    def edge(g):
        return [v[0] for v in split_wide(edge_h, g, 1, main)]

    inner_stencil(column, edge, cols, count, here, start)


def split_wide(ref, start, size, main):
    return [ref[start : start + size, :, :main], ref[start : start + size, :, main:]]


def residual(source, totals, cols, main, r, keep=None):
    for c in range(0, cols, CHUNK):
        x = source(c)
        sums = [frame_sum(total, c, cols, main, base) for total, base in totals]
        value = [x[0] + s[0] for s in sums] + [beside(x[1] + sums[0][1], x[1] + sums[1][1])]
        lane, size = 0, CHUNK * SUB
        for v in value:
            width = v.shape[-1]
            v = v.reshape(size, width)
            if keep is not None:
                v = jnp.where(keep, v, 0.0)
            r[c * SUB : c * SUB + size, lane : lane + width] = v.astype(BF16)
            lane += width


def second_convolution(flags, spread, conds, cols, count, main, weight, tails, edge_h, here, there, total):
    size, step = cols * SUB, cols * SUB + PAD

    @stage(flags)
    def _():
        hidden_stencil(flags, spread, conds[0], cols, count, main, edge_h.at[0], here, 0)

    @stage(flags)
    def _():
        convolve(here, weight, tails, total, 0, size, main)
        hidden_stencil(flags, spread, conds[1], cols, count, main, edge_h.at[1], there, 0)

    @stage(flags)
    def _():
        convolve(there, weight, tails, total, 0, size, main, step)

    return [(total, 0), (total, step)]


def columns(video, f, main):
    return lambda c, size=CHUNK: split(video[f, c : c + size].astype(F32), main)


def prepare_kernel(main, flags, raw, video, edge, sent):
    cols = video.shape[1]
    half, count = cols // 2, cols // 4
    for f in range(2):
        for c in range(0, cols, CHUNK):
            store(video.at[f], c, split(raw[f, c : c + CHUNK], main))
    far = columns(video, flags[FAR], main)
    for c in range(0, half, CHUNK):
        low, high = far(c), far(half + c)
        value = jnp.concatenate([low[0], high[0], beside(low[1], high[1])], axis=-1)
        sent[c : c + CHUNK] = value.astype(BF16)
    for i, which in enumerate((NEAR, FAR)):
        column = columns(video, flags[which], main)
        tile = edges_of(lambda c: [v[0] for v in column(c, 1)], count)
        for g in range(count):
            for k, value in enumerate(tile(g)):
                store(edge, (2 * k + i) * count + g, [v[None] for v in value])


def first_stencil(flags, video, which, slot, own, up, down, main, here):
    cols = video.shape[1]
    count, step = cols // 4, cols * SUB + PAD
    slots = own.shape[0] // (2 * count)

    def at(ref):
        return lambda k, g: [v[0] for v in split(ref[pl.ds((slots * k + slot) * count + g, 1)].astype(F32), main)]

    nearby = edge_stencil(flags, lambda g: at(own)(0, g), at(up), at(down), count, main, here, step)
    inner_stencil(columns(video, flags[which], main), lambda g: nearby[g], cols, count, here)


def near_kernel(
    main, flags, video, own, up, down, start, end, first, second,
    r, tails_first, tails_second, here, there, total, spread, edge_h,
):
    cols = video.shape[1]
    count, step = cols // 4, cols * SUB + PAD
    rows = step + (count + count % 2) * SUB

    pack_tails(first, tails_first, main)
    first_stencil(flags, video, NEAR, 0, own, up, down, main, here)

    pack_tails(second, tails_second, main)

    @stage(flags)
    def _():
        convolve(here, first, tails_first, total, 0, rows, main)

    spread_halves(total, spread, cols, count, main, 0, step)
    totals = second_convolution(
        flags, spread, (start, end), cols, count, main, second, tails_second, edge_h, here, there, total
    )
    residual(columns(video, flags[NEAR], main), totals, cols, main, r)


def relay_kernel(main, got, edge):
    half = got.shape[0]
    count = half // 2
    tile = edges_of(lambda c: [v[0] for v in unpack(got[c % half : c % half + 1].astype(F32), main, c // half)], count)
    for g in range(count):
        for k, value in enumerate(tile(g)):
            store(edge, k * count + g, [v[None] for v in value])


def got_columns(got, main):
    half = got.shape[0]
    return lambda c: unpack(got[c % half : c % half + CHUNK].astype(F32), main, c // half)


def other_kernel(
    main, flags, video, own, up, down, start, end, first, tails_first, second, tails_second,
    r, here, there, total, spread, edge_h,
):
    cols = video.shape[1]
    count, step = cols // 4, cols * SUB + PAD
    rows = step + (count + count % 2) * SUB
    first_stencil(flags, video, FAR, 1, own, up, down, main, here)

    @stage(flags)
    def _():
        convolve(here, first, tails_first, total, 0, rows, main)

    spread_halves(total, spread, cols, count, main, 0, step)

    totals = second_convolution(
        flags, spread, (start, end), cols, count, main, second, tails_second, edge_h, here, there, total
    )
    residual(columns(video, flags[FAR], main), totals, cols, main, r)


def mix(sources, taps, main, p):
    left = [r[:, p * main : (p + 1) * main] for r, _ in sources] + [r[:, 2 * main :] for r, _ in sources]
    right = [taps[t, :main] for _, t in sources]
    for _, t in sources:
        tail = taps[t, main:]
        right += [tail, jnp.zeros_like(tail)] if p == 0 else [jnp.zeros_like(tail), tail]
    return jnp.dot(jnp.concatenate(left, axis=1), jnp.concatenate(right, axis=0), preferred_element_type=F32)


def blend(r, mixed, start, size, main):
    value = r[start : start + size].astype(F32)
    both = [unpack(value, main, p) for p in range(2)]
    out = []
    for i in range(2):
        part = None
        for p in range(2):
            t = 0.5 * mixed(p, start, size)[i]
            term = both[p][i] + half_silu(t)
            part = term if part is None else part + term
        out.append(0.5 * part)
    return out


def far_kernel(
    main, flags, got, own, up, down, start, end, first, tails_first, second, tails_second, r_near, r_far, taps,
    out, mixed, here, there, total, spread, edge_h, r, sums,
):
    half = got.shape[0]
    cols = 2 * half
    count, size = half // 2, cols * SUB
    step = size + PAD
    rows = step + (count + count % 2) * SUB

    def at(ref):
        return lambda k, g: [v[0] for v in split(ref[k * count + g : k * count + g + 1].astype(F32), main)]

    nearby = edge_stencil(flags, lambda g: at(own)(0, g), at(up), at(down), count, main, here, step)
    inner_stencil(got_columns(got, main), lambda g: nearby[g], cols, count, here)
    convolve(here, first, tails_first, total, 0, rows, main)
    spread_halves(total, spread, cols, count, main, 0, step)
    to_far, to_near = flags[TAP_FAR], flags[TAP_NEAR]
    toward = [(to_far, to_near), (to_near, to_far)]
    totals = second_convolution(
        flags, spread, (start, end), cols, count, main, second, tails_second, edge_h, here, there, total
    )

    @stage(flags)
    def _():
        for p in range(2):
            mixed[p] = mix([(r_far, toward[p][0]), (r_near, 1)], taps, main, p)
        residual(got_columns(got, main), totals, cols, main, r, flags[HAS_FAR] > 0)

    @stage(flags)
    def _():
        for p in range(2):
            sums[p] = mix([(r, toward[p][0]), (r_far, 1), (r_near, toward[p][1])], taps, main, p)

    piece = CHUNK * SUB
    for s in range(0, size, piece):
        value = blend(r_far, lambda p, a, n: split(sums[p, a : a + n], main), s, piece, main)
        store(out, s // SUB, [v.reshape(CHUNK, SUB, v.shape[-1]) for v in value])


def last_kernel(main, parts, flags, got, mixed, r_near, taps, done, out, staged, sums, sems):
    cols = done.shape[0]
    copies = [pltpu.make_async_copy(done, out.at[flags[FAR]], sems.at[parts])]
    copies[0].start()
    toward = [flags[TAP_NEAR], flags[TAP_FAR]]
    for p in range(2):
        sums[p] = mixed[p] + mix([(got, toward[p])], taps, main, p)
    piece = CHUNK * SUB
    for i in range(parts):
        first, last = i * cols // parts, (i + 1) * cols // parts

        @stage(flags)
        def _():
            for c in range(first, last, CHUNK):
                value = blend(r_near, lambda p, a, n: split(sums[p, a : a + n], main), c * SUB, piece, main)
                store(staged, c, [v.reshape(CHUNK, SUB, v.shape[-1]) for v in value])

        copy = pltpu.make_async_copy(
            staged.at[first:last], out.at[flags[NEAR], first:last], sems.at[i]
        )
        copy.start()
        copies.append(copy)
    for copy in copies:
        copy.wait()


VMEM = pl.BlockSpec(memory_space=pltpu.VMEM)
SMEM = pl.BlockSpec(memory_space=pltpu.SMEM)
HBM = pl.BlockSpec(memory_space=pltpu.HBM)


def call(kernel, outs, args, scratch=(), name=None, flops=0, out_specs=None, limit=24):
    return pl.pallas_call(
        kernel,
        out_shape=outs,
        in_specs=[SMEM if a.dtype == jnp.int32 else VMEM for a in args],
        out_specs=out_specs or jax.tree.map(lambda _: VMEM, outs),
        scratch_shapes=list(scratch),
        name=name,
        cost_estimate=pl.CostEstimate(flops=flops, bytes_accessed=1 << 20, transcendentals=0),
        compiler_params=pltpu.CompilerParams(vmem_limit_bytes=limit << 20),
    )(*args)


def pairs(count, start):
    links = [(i, i + 1) for i in range(start, count - 1, 2)]
    return links + [(b, a) for a, b in links]


def row_neighbours(edge):
    count = lax.axis_size("row")
    if count == 1:
        return edge, edge
    first = lax.ppermute(edge, "row", pairs(count, 0))
    if count == 2:
        return first, first
    second = lax.ppermute(edge, "row", pairs(count, 1))
    even = lax.axis_index("row") % 2 == 0
    return jnp.where(even, second, first), jnp.where(even, first, second)


def shards(latents, conv_first, conv_second, conv_time, cond_start, cond_end):
    _, rows, cols, channels = latents.shape
    main = channels // LANES * LANES
    assert latents.shape[0] == 2 and rows == SUB and 2 * (channels - main) == LANES and cols % 4 == 0
    pixels, count = rows * cols, cols // 4
    step = pixels + PAD
    width = 3 * main + 2 * LANES
    wide = main + 2 * LANES
    packed = 2 * main + LANES
    frames_n, rows_n = lax.axis_size("frame"), lax.axis_size("row")
    frame, row = lax.axis_index("frame"), lax.axis_index("row")
    odd = frame % 2
    has_far = jnp.where(odd == 1, frame < frames_n - 1, frame > 0)
    flags = jnp.stack([1 - odd, odd, 2 * odd, 2 - 2 * odd, has_far, row > 0, row < rows_n - 1]).astype(jnp.int32)
    video = jnp.transpose(latents, (0, 2, 1, 3))
    unit = 32 * pixels * LANES * LANES

    def struct(*shape, dtype=BF16):
        return jax.ShapeDtypeStruct(shape, dtype)

    here, there = (step + (count + 3) * SUB, width), (step, width)
    work = [
        pltpu.VMEM(here, BF16), pltpu.VMEM(there, BF16), pltpu.VMEM((2 * step, wide), F32),
        pltpu.VMEM((cols + count, SUB, main + LANES), F32), pltpu.VMEM((2, count, SUB, main + LANES), F32),
    ]
    video, edge, sent = call(
        functools.partial(prepare_kernel, main),
        (struct(2, cols, SUB, main + LANES), struct(4 * count, SUB, main + LANES), struct(cols // 2, SUB, packed)),
        (flags, video), name="prepare", flops=8 * unit,
    )
    up, down = row_neighbours(edge)
    got_far = lax.ppermute(sent, "frame", pairs(frames_n, 1))
    first, second, taps = conv_first, conv_second, conv_time
    r_near, tails_first, tails_second = call(
        functools.partial(near_kernel, main),
        (struct(pixels, packed), struct(width, 2 * LANES), struct(width, 2 * LANES)),
        (flags, video, edge, up, down, cond_start, cond_end, first, second), work, "near", 54 * unit,
    )
    got_near = lax.ppermute(r_near, "frame", pairs(frames_n, 0))
    got_far, _ = lax.optimization_barrier((got_far, r_near))
    far_edge = call(functools.partial(relay_kernel, main), struct(2 * count, SUB, main + LANES), (got_far,), name="relay")
    far_up, far_down = row_neighbours(far_edge)
    r_far = call(
        functools.partial(other_kernel, main), struct(pixels, packed),
        (flags, video, edge, up, down, cond_start, cond_end, first, tails_first, second, tails_second),
        work, "other", 54 * unit,
    )
    done, mixed = call(
        functools.partial(far_kernel, main), (struct(cols, SUB, channels), struct(2, pixels, channels, dtype=F32)),
        (
            flags, got_far, far_edge, far_up, far_down, cond_start, cond_end, first, tails_first, second,
            tails_second, r_near, r_far, taps,
        ),
        [*work, pltpu.VMEM((pixels, packed), BF16), pltpu.VMEM((2, pixels, channels), F32)], "far", 54 * unit,
    )
    parts = 3
    out = call(
        functools.partial(last_kernel, main, parts), struct(2, cols, SUB, channels),
        (flags, got_near, mixed, r_near, taps, done),
        [
            pltpu.VMEM((cols, SUB, channels), BF16), pltpu.VMEM((2, pixels, channels), F32),
            pltpu.SemaphoreType.DMA((parts + 1,)),
        ],
        "last", 4 * unit, HBM,
    )
    return jnp.transpose(out, (0, 2, 1, 3))


def solution(mesh):
    placed = (P("frame", "row", None, None), P(), P(), P(), P(), P())
    return jax.shard_map(
        shards, mesh=mesh, in_specs=placed, out_specs=P("frame", "row", None, None), check_vma=False
    )
```

time: 55.6 us -> 25 us (0.45)
  the two profiles are of different devices: /device:TPU:0 before, /device:TPU:15 now
where the time goes in v2:
time: 25 us; the launch traced here: 24.9 us
  Pallas kernels  16.3 us (65%)
  starting transfers between devices  5.22 us (21%)
  waiting for transfers between devices  2.17 us (9%)
  local copies, waits for them, and re-layouts  1.12 us (4%)
    pallas_call x6, Pallas kernels, call(): pl.pallas_call(kernel, out_shape=outs, in_specs=[SMEM if a.dtype == jnp.i...  16.3 us
    ppermute x1, starting transfers between devices, shards(): got_far = lax.ppermute(sent, 'frame', pairs(frames_n, 1))  3.11 us
    ppermute x1, waiting for transfers between devices, shards(): got_far = lax.ppermute(sent, 'frame', pairs(frames_n, 1))  2.16 us
    ppermute x2, starting transfers between devices, row_neighbours(): first = lax.ppermute(edge, 'row', pairs(count, 0))  1.85 us
    unnamed x12, local copies, waits for them, and re-layouts  1.03 us
  transfers between devices with their start and end apart: 4, of which 1 were waited for; matrix products, arithmetic and copies ran while one was open for 0% of the time, Pallas kernels for 54%

profile of v2, /device:TPU:15, one launch (start us, length us, event | category | flops | bytes accessed | tf_op | source)
XLA Modules:
  0.0 24.9 jit_solution(15240969941106208036)
XLA Ops:
  0.0 0.1 stack.43.flags
  0.1 0.0 copy-start.3
  0.1 1.0 %copy-done.3 = bf16[2,8,36,320]{3,1,2,0:T(8,128)(2,1)S(1)} copy-done((bf16[2,8,36,320]{3,1,2,0:T(8,128)(2,1)S(1)}, bf16[2,8,36,320]{3,1,2,0:T(8,128)(2,1)}, u32[]{:S(2)}) %copy-start.3) | copy-done | bytes 368664
  1.1 0.0 copy-start.1
  1.1 0.0 copy-start.2
  1.1 0.8 %prepare.1 = (bf16[2,36,8,384]{3,2,1,0:T(8,128)(2,1)S(1)}, bf16[36,8,384]{2,1,0:T(8,128)(2,1)S(1)}, bf16[18,8,640]{2,1,0:T(8,128)(2,1)S(1)}) custom-call(s32[7]{0:T(128)S(1)} %stack.43.flags, bf16[2,36,8,320]{3,2,1,0:T(8,128)(2,1)S(1)} %bitcast.9), custom_call_target="tpu_custom_call" | custom-call | flops 1207959552 | bytes 1048576 | tf_op jit(solution)/shard_map/prepare/pallas_call | solution.py:471
  1.9 0.7 %collective-permute-start = (bf16[36,8,384]{2,1,0:T(8,128)(2,1)S(1)}, bf16[36,8,384]{2,1,0:T(8,128)(2,1)S(1)}, u32[]{:S(2)}, u32[]{:S(2)}) collective-permute-start(bf16[36,8,384]{2,1,0:T(8,128)(2,1)S(1)} %get-tuple-element.15.own), channel_id=1, source_target_pairs={{0,1},{1,0},{2,3},{3,2},{4,5},{5,4},{6,7},{7,6},{8,9},{9,8},{10,11... | collective-permute-start | bytes 663560 | tf_op jit(solution)/shard_map/ppermute | solution.py:492
  2.7 3.1 %collective-permute-start.2 = (bf16[18,8,640]{2,1,0:T(8,128)(2,1)S(1)}, bf16[18,8,640]{2,1,0:T(8,128)(2,1)S(1)}, u32[]{:S(2)}, u32[]{:S(2)}) collective-permute-start(bf16[18,8,640]{2,1,0:T(8,128)(2,1)S(1)} %get-tuple-element.17), channel_id=1, source_target_pairs={{2,4},{6,8},{10,12},{14,16},{18,20},{22,24},{26,28},{4,2},{8,6},{1... | collective-permute-start | bytes 552968 | tf_op jit(solution)/shard_map/ppermute | solution.py:531
  5.8 0.0 collective-permute-done.up.down
  5.8 0.0 copy-done.1
  5.8 0.0 copy-done.2
  5.8 0.0 copy-done.4
  5.8 0.0 copy-done.5
  5.8 4.1 %near.1 = (bf16[288,640]{1,0:T(8,128)(2,1)S(1)}, bf16[1024,256]{1,0:T(8,128)(2,1)S(1)}, bf16[1024,256]{1,0:T(8,128)(2,1)S(1)}) custom-call(s32[7]{0:T(128)S(1)} %stack.43.flags, bf16[2,36,8,384]{3,2,1,0:T(8,128)(2,1)S(1)} %get-tuple-element.14.video, bf16[36,8,384]{2,1,0:T(8,128)(2,1)S(1)} %get-tuple-element.15.own, ...), custom_call_target="tpu_custom_call" | custom-call | flops 8153726976 | bytes 1048576 | tf_op jit(solution)/shard_map/near/pallas_call | solution.py:471
  10.0 0.3 %collective-permute-start.1 = (bf16[288,640]{1,0:T(8,128)(2,1)S(1)}, bf16[288,640]{1,0:T(8,128)(2,1)S(1)}, u32[]{:S(2)}, u32[]{:S(2)}) collective-permute-start(bf16[288,640]{1,0:T(8,128)(2,1)S(1)} %get-tuple-element.16.r_near), channel_id=1, source_target_pairs={{0,2},{4,6},{8,10},{12,14},{16,18},{20,22},{24,26},{28,30},{2,0},{... | collective-permute-start | bytes 1105928 | tf_op jit(solution)/shard_map/ppermute | solution.py:538
  10.2 2.2 %collective-permute-done.2.got = bf16[18,8,640]{2,1,0:T(8,128)(2,1)S(1)} collective-permute-done((bf16[18,8,640]{2,1,0:T(8,128)(2,1)S(1)}, bf16[18,8,640]{2,1,0:T(8,128)(2,1)S(1)}, u32[]{:S(2)}, u32[]{:S(2)}) %collective-permute-start.2) | collective-permute-done | bytes 184352 | tf_op jit(solution)/shard_map/ppermute | solution.py:531
  12.4 0.1 relay.1.own
  12.5 1.1 %collective-permute-start.3 = (bf16[18,8,384]{2,1,0:T(8,128)(2,1)S(1)}, bf16[18,8,384]{2,1,0:T(8,128)(2,1)S(1)}, u32[]{:S(2)}, u32[]{:S(2)}) collective-permute-start(bf16[18,8,384]{2,1,0:T(8,128)(2,1)S(1)} %relay.1.own), channel_id=1, source_target_pairs={{0,1},{1,0},{2,3},{3,2},{4,5},{5,4},{6,7},{7,6},{8,9},{9,8},{10,11... | collective-permute-start | bytes 331784 | tf_op jit(solution)/shard_map/ppermute | solution.py:492
  13.6 4.0 %other.1.r_far = bf16[288,640]{1,0:T(8,128)(2,1)S(1)} custom-call(s32[7]{0:T(128)S(1)} %stack.43.flags, bf16[2,36,8,384]{3,2,1,0:T(8,128)(2,1)S(1)} %get-tuple-element.14.video, bf16[36,8,384]{2,1,0:T(8,128)(2,1)S(1)} %get-tuple-element.15.own, bf16[36,8,384]{2,1,0:T(8,128)(2,1)S(1)} %collective-permute-done.up.down, ...), custom_call_target="tpu_custom_call" | custom-call | flops 8153726976 | bytes 1048576 | tf_op jit(solution)/shard_map/other/pallas_call | solution.py:471
  17.6 0.0 collective-permute-done.3.up.down
  17.6 0.0 copy-done
  17.6 5.3 %far.1 = (bf16[36,8,320]{2,1,0:T(8,128)(2,1)S(1)}, f32[2,288,320]{2,1,0:T(8,128)S(1)}) custom-call(s32[7]{0:T(128)S(1)} %stack.43.flags, bf16[18,8,640]{2,1,0:T(8,128)(2,1)S(1)} %collective-permute-done.2.got, bf16[18,8,384]{2,1,0:T(8,128)(2,1)S(1)} %relay.1.own, bf16[18,8,384]{2,1,0:T(8,128)(2,1)S(1)} %collective-permute-done.3.up.down, ...), custom_call_target="tpu_custom_call" | custom-call | flops 8153726976 | bytes 1048576 | tf_op jit(solution)/shard_map/far/pallas_call | solution.py:471
  23.0 0.0 collective-permute-done.1.got
  23.0 1.9 %last.1 = bf16[2,36,8,320]{3,2,1,0:T(8,128)(2,1)} custom-call(s32[7]{0:T(128)S(1)} %stack.43.flags, bf16[288,640]{1,0:T(8,128)(2,1)S(1)} %collective-permute-done.1.got, f32[2,288,320]{2,1,0:T(8,128)S(1)} %get-tuple-element.21.mixed, bf16[288,640]{1,0:T(8,128)(2,1)S(1)} %get-tuple-element.16.r_near, bf16[3,320,320]{2,1,0:T(8,128)(2,1)S(1)} %copy-done, ...), custom_call_target="tpu_custom_call" | custom-call | flops 603979776 | bytes 1048576 | tf_op jit(solution)/shard_map/last/pallas_call | solution.py:471
  (3 shorter events, 0.0 us)
Async XLA Ops:
  0.1 1.0 %copy-start.3 = (bf16[2,8,36,320]{3,1,2,0:T(8,128)(2,1)S(1)}, bf16[2,8,36,320]{3,1,2,0:T(8,128)(2,1)}, u32[]{:S(2)}) copy-start(bf16[2,8,36,320]{3,1,2,0:T(8,128)(2,1)} %param.6) | copy-start | bytes 1105924
  1.1 4.7 %copy-start.1 = (bf16[3,3,320,320]{3,2,1,0:T(8,128)(2,1)S(1)}, bf16[3,3,320,320]{3,2,1,0:T(8,128)(2,1)}, u32[]{:S(2)}) copy-start(bf16[3,3,320,320]{3,2,1,0:T(8,128)(2,1)} %first.5) | copy-start | bytes 5529604
  1.1 4.7 %copy-start.2 = (bf16[3,3,320,320]{3,2,1,0:T(8,128)(2,1)S(1)}, bf16[3,3,320,320]{3,2,1,0:T(8,128)(2,1)}, u32[]{:S(2)}) copy-start(bf16[3,3,320,320]{3,2,1,0:T(8,128)(2,1)} %second.5) | copy-start | bytes 5529604
  1.1 4.7 %copy-start.4 = (f32[320]{0:T(512)S(1)}, f32[320]{0:T(512)}, u32[]{:S(2)}) copy-start(f32[320]{0:T(512)} %start.5) | copy-start | bytes 3844
  1.1 4.7 %copy-start.5 = (f32[320]{0:T(512)S(1)}, f32[320]{0:T(512)}, u32[]{:S(2)}) copy-start(f32[320]{0:T(512)} %end.5) | copy-start | bytes 3844
  1.9 3.9 %collective-permute-start = (bf16[36,8,384]{2,1,0:T(8,128)(2,1)S(1)}, bf16[36,8,384]{2,1,0:T(8,128)(2,1)S(1)}, u32[]{:S(2)}, u32[]{:S(2)}) collective-permute-start(bf16[36,8,384]{2,1,0:T(8,128)(2,1)S(1)} %get-tuple-element.15.own), channel_id=1, source_target_pairs={{0,1},{1,0},{2,3},{3,2},{4,5},{5,4},{6,7},{7,6},{8,9},{9,8},{10,11... | collective-permute-start | bytes 663560 | tf_op jit(solution)/shard_map/ppermute | solution.py:492
  2.7 9.7 %collective-permute-start.2 = (bf16[18,8,640]{2,1,0:T(8,128)(2,1)S(1)}, bf16[18,8,640]{2,1,0:T(8,128)(2,1)S(1)}, u32[]{:S(2)}, u32[]{:S(2)}) collective-permute-start(bf16[18,8,640]{2,1,0:T(8,128)(2,1)S(1)} %get-tuple-element.17), channel_id=1, source_target_pairs={{2,4},{6,8},{10,12},{14,16},{18,20},{22,24},{26,28},{4,2},{8,6},{1... | collective-permute-start | bytes 552968 | tf_op jit(solution)/shard_map/ppermute | solution.py:531
  10.0 13.0 %collective-permute-start.1 = (bf16[288,640]{1,0:T(8,128)(2,1)S(1)}, bf16[288,640]{1,0:T(8,128)(2,1)S(1)}, u32[]{:S(2)}, u32[]{:S(2)}) collective-permute-start(bf16[288,640]{1,0:T(8,128)(2,1)S(1)} %get-tuple-element.16.r_near), channel_id=1, source_target_pairs={{0,2},{4,6},{8,10},{12,14},{16,18},{20,22},{24,26},{28,30},{2,0},{... | collective-permute-start | bytes 1105928 | tf_op jit(solution)/shard_map/ppermute | solution.py:538
  12.5 5.1 %collective-permute-start.3 = (bf16[18,8,384]{2,1,0:T(8,128)(2,1)S(1)}, bf16[18,8,384]{2,1,0:T(8,128)(2,1)S(1)}, u32[]{:S(2)}, u32[]{:S(2)}) collective-permute-start(bf16[18,8,384]{2,1,0:T(8,128)(2,1)S(1)} %relay.1.own), channel_id=1, source_target_pairs={{0,1},{1,0},{2,3},{3,2},{4,5},{5,4},{6,7},{7,6},{8,9},{9,8},{10,11... | collective-permute-start | bytes 331784 | tf_op jit(solution)/shard_map/ppermute | solution.py:492
  13.6 4.0 %copy-start = (bf16[3,320,320]{2,1,0:T(8,128)(2,1)S(1)}, bf16[3,320,320]{2,1,0:T(8,128)(2,1)}, u32[]{:S(2)}) copy-start(bf16[3,320,320]{2,1,0:T(8,128)(2,1)} %taps.3) | copy-start | bytes 1843204

commit v3 on v2

--- a/solution.py
+++ b/solution.py
@@ -116,11 +116,26 @@
         return here[first : first + size]
 
     rows = slice(into, into + size)
-    out = jnp.dot(left(1), taps(1), preferred_element_type=F32)
-    out += jnp.dot(left(0), taps(0), preferred_element_type=F32)
-    out += jnp.dot(left(2), taps(2), preferred_element_type=F32)
-    total[rows, :main] = out
-    total[rows, main:] = jnp.dot(left(1), tails[...], preferred_element_type=F32)
+
+    def two():
+        total[rows, :main] = jnp.dot(left(1), taps(1), preferred_element_type=F32) + jnp.dot(
+            left(0), taps(0), preferred_element_type=F32
+        )
+
+    def one():
+        total[rows, main : 2 * main] = jnp.dot(left(2), taps(2), preferred_element_type=F32)
+
+    def last():
+        total[rows, 2 * main :] = jnp.dot(left(1), tails[...], preferred_element_type=F32)
+
+    return [two, one, last]
+
+
+def weave(some, others=()):
+    for i, step in enumerate(some):
+        step()
+        for other in others[i * len(others) // len(some) : (i + 1) * len(others) // len(some)]:
+            other()
 
 
 def tail_of(left, mid, right):
@@ -131,26 +146,24 @@
     out, tail = [], []
     for i in range(c, c + CHUNK):
         s = base + i * SUB
-        mid = total[s : s + SUB, main:]
-        left = total[s - SUB : s, main:] if i > 0 else jnp.zeros_like(mid)
-        right = total[s + SUB : s + 2 * SUB, main:] if i < cols - 1 else jnp.zeros_like(mid)
-        out.append(total[s : s + SUB, :main])
+        mid = total[s : s + SUB, 2 * main :]
+        left = total[s - SUB : s, 2 * main :] if i > 0 else jnp.zeros_like(mid)
+        right = total[s + SUB : s + 2 * SUB, 2 * main :] if i < cols - 1 else jnp.zeros_like(mid)
+        out.append(total[s : s + SUB, :main] + total[s : s + SUB, main : 2 * main])
         tail.append(tail_of(left, mid, right))
     return [jnp.stack(out), jnp.stack(tail)]
 
 
 def edge_sum(total, g, count, main, base):
-    mid = total[base + g * SUB : base + (g + 1) * SUB, main:]
+    def tile(i, part):
+        return total[base + i * SUB : base + (i + 1) * SUB, part]
+
+    tail = slice(2 * main, None)
+    mid = tile(g, tail)
     row = rows_of(mid)
-    if g > 0:
-        left = total[base + (g - 1) * SUB : base + g * SUB, main:]
-    else:
-        left = jnp.where((row == 7) | (row == 0), 0.0, turn(total[base + (count - 1) * SUB : base + count * SUB, main:], 2))
-    if g < count - 1:
-        right = total[base + (g + 1) * SUB : base + (g + 2) * SUB, main:]
-    else:
-        right = jnp.where((row == 5) | (row == 6), 0.0, turn(total[base : base + SUB, main:], -2))
-    return [total[base + g * SUB : base + (g + 1) * SUB, :main], tail_of(left, mid, right)]
+    left = tile(g - 1, tail) if g > 0 else jnp.where((row == 7) | (row == 0), 0.0, turn(tile(count - 1, tail), 2))
+    right = tile(g + 1, tail) if g < count - 1 else jnp.where((row == 5) | (row == 6), 0.0, turn(tile(0, tail), -2))
+    return [tile(g, slice(0, main)) + tile(g, slice(main, 2 * main)), tail_of(left, mid, right)]
 
 
 def edge_stencil(flags, outer, up, down, count, main, here, start):
@@ -186,8 +199,8 @@
 
 def inner_stencil(column, edge, cols, count, here, start=0):
     stencil = Stencil(here, start)
-    blank = None
-    for c in range(0, cols, CHUNK):
+
+    def add(c):
         mid = column(c)
         outer = [[turn(v, -2 * (i // count)) for v in edge(i % count)] for i in range(c, c + CHUNK)]
         prev, nxt = [], []
@@ -196,11 +209,13 @@
             prev.append(turn(jnp.where(rows_of(v) == 7, e, v), 1))
             nxt.append(turn(jnp.where(rows_of(v) == 0, e, v), -1))
         pieces = Stencil.pieces(prev, mid, nxt)
-        if blank is None:
-            blank = [jnp.zeros_like(p[:1]) for p in pieces]
-            stencil.put(blank)
+        if c == 0:
+            stencil.put([jnp.zeros_like(p[:1]) for p in pieces])
         stencil.put(pieces)
-    stencil.put(blank)
+        if c == cols - CHUNK:
+            stencil.put([jnp.zeros_like(p[:1]) for p in pieces])
+
+    return [functools.partial(add, c) for c in range(0, cols, CHUNK)]
 
 
 def half_silu(y):
@@ -224,13 +239,11 @@
 
 def hidden_stencil(flags, spread, cond, cols, count, main, edge_h, here, start):
     halves = cond_halves(cond, main)
-    for g in range(count):
+
+    def outside(g):
         h = [half_silu(v + b) for v, b in zip(split_wide(spread, cols + g, 1, main), halves)]
         above = [lax.rem(rows_of(v), 2) == 1 for v in h]
-        h = [
-            jnp.where(jnp.where(a, flags[HAS_UP], flags[HAS_DOWN]) > 0, v, 0.0) for v, a in zip(h, above)
-        ]
-        store(edge_h, g, h)
+        store(edge_h, g, [jnp.where(jnp.where(a, flags[HAS_UP], flags[HAS_DOWN]) > 0, v, 0.0) for v, a in zip(h, above)])
 
     def column(c):
         return [half_silu(v + b) for v, b in zip(split_wide(spread, c, CHUNK, main), halves)]
@@ -238,7 +251,7 @@
     def edge(g):
         return [v[0] for v in split_wide(edge_h, g, 1, main)]
 
-    inner_stencil(column, edge, cols, count, here, start)
+    return [functools.partial(outside, g) for g in range(count)] + inner_stencil(column, edge, cols, count, here, start)
 
 
 def split_wide(ref, start, size, main):
@@ -260,21 +273,14 @@
             lane += width
 
 
-def second_convolution(flags, spread, conds, cols, count, main, weight, tails, edge_h, here, there, total):
-    size, step = cols * SUB, cols * SUB + PAD
+def second_convolution(flags, spread, conds, cols, count, main, weight, tails, edge_h, here, total):
+    step = cols * SUB + PAD
+    for p in range(2):
+        weave(hidden_stencil(flags, spread, conds[p], cols, count, main, edge_h.at[p], here, p * step))
 
     @stage(flags)
     def _():
-        hidden_stencil(flags, spread, conds[0], cols, count, main, edge_h.at[0], here, 0)
-
-    @stage(flags)
-    def _():
-        convolve(here, weight, tails, total, 0, size, main)
-        hidden_stencil(flags, spread, conds[1], cols, count, main, edge_h.at[1], there, 0)
-
-    @stage(flags)
-    def _():
-        convolve(there, weight, tails, total, 0, size, main, step)
+        weave(convolve(here, weight, tails, total, 0, step + cols * SUB, main))
 
     return [(total, 0), (total, step)]
 
@@ -311,29 +317,29 @@
         return lambda k, g: [v[0] for v in split(ref[pl.ds((slots * k + slot) * count + g, 1)].astype(F32), main)]
 
     nearby = edge_stencil(flags, lambda g: at(own)(0, g), at(up), at(down), count, main, here, step)
-    inner_stencil(columns(video, flags[which], main), lambda g: nearby[g], cols, count, here)
+    return inner_stencil(columns(video, flags[which], main), lambda g: nearby[g], cols, count, here)
 
 
 def near_kernel(
     main, flags, video, own, up, down, start, end, first, second,
-    r, tails_first, tails_second, here, there, total, spread, edge_h,
+    r, tails_first, tails_second, here, total, spread, edge_h,
 ):
     cols = video.shape[1]
     count, step = cols // 4, cols * SUB + PAD
     rows = step + (count + count % 2) * SUB
 
     pack_tails(first, tails_first, main)
-    first_stencil(flags, video, NEAR, 0, own, up, down, main, here)
+    weave(first_stencil(flags, video, NEAR, 0, own, up, down, main, here))
 
     pack_tails(second, tails_second, main)
 
     @stage(flags)
     def _():
-        convolve(here, first, tails_first, total, 0, rows, main)
+        weave(convolve(here, first, tails_first, total, 0, rows, main))
 
     spread_halves(total, spread, cols, count, main, 0, step)
     totals = second_convolution(
-        flags, spread, (start, end), cols, count, main, second, tails_second, edge_h, here, there, total
+        flags, spread, (start, end), cols, count, main, second, tails_second, edge_h, here, total
     )
     residual(columns(video, flags[NEAR], main), totals, cols, main, r)
 
@@ -354,21 +360,21 @@
 
 def other_kernel(
     main, flags, video, own, up, down, start, end, first, tails_first, second, tails_second,
-    r, here, there, total, spread, edge_h,
+    r, here, total, spread, edge_h,
 ):
     cols = video.shape[1]
     count, step = cols // 4, cols * SUB + PAD
     rows = step + (count + count % 2) * SUB
-    first_stencil(flags, video, FAR, 1, own, up, down, main, here)
+    weave(first_stencil(flags, video, FAR, 1, own, up, down, main, here))
 
     @stage(flags)
     def _():
-        convolve(here, first, tails_first, total, 0, rows, main)
+        weave(convolve(here, first, tails_first, total, 0, rows, main))
 
     spread_halves(total, spread, cols, count, main, 0, step)
 
     totals = second_convolution(
-        flags, spread, (start, end), cols, count, main, second, tails_second, edge_h, here, there, total
+        flags, spread, (start, end), cols, count, main, second, tails_second, edge_h, here, total
     )
     residual(columns(video, flags[FAR], main), totals, cols, main, r)
 
@@ -382,23 +388,47 @@
     return jnp.dot(jnp.concatenate(left, axis=1), jnp.concatenate(right, axis=0), preferred_element_type=F32)
 
 
+def mix_kernel(main, flags, r_near, r_far, taps, mixed):
+    toward = [(flags[TAP_FAR], flags[TAP_NEAR]), (flags[TAP_NEAR], flags[TAP_FAR])]
+    for p in range(2):
+        to_far, to_near = toward[p]
+        left = [r[:, part] for part in (slice(p * main, (p + 1) * main), slice(2 * main, None)) for r in (r_far, r_near)]
+
+        pairs_of = [(taps[1], taps[to_far]), (taps[to_near], taps[1])]
+
+        def right(column):
+            parts = [column(a[:main], b[:main]) for a, b in pairs_of]
+            for tail in [column(a[main:], b[main:]) for a, b in pairs_of]:
+                blank = jnp.zeros_like(tail)
+                parts += [tail, blank] if p == 0 else [blank, tail]
+            return jnp.concatenate(parts, axis=0)
+
+        value = jnp.concatenate(left, axis=1)
+        columns_of = [
+            lambda a, b: a[:, :main], lambda a, b: b[:, :main], lambda a, b: jnp.concatenate([a[:, main:], b[:, main:]], axis=1)
+        ]
+        for k, column in enumerate(columns_of):
+            part = jnp.dot(value, right(column), preferred_element_type=F32)
+            mixed[p, :, k * main : k * main + part.shape[1]] = part
+
+
 def blend(r, mixed, start, size, main):
     value = r[start : start + size].astype(F32)
     both = [unpack(value, main, p) for p in range(2)]
-    out = []
-    for i in range(2):
-        part = None
-        for p in range(2):
-            t = 0.5 * mixed(p, start, size)[i]
-            term = both[p][i] + half_silu(t)
-            part = term if part is None else part + term
-        out.append(0.5 * part)
-    return out
+    terms = [mixed(p, start, size) for p in range(2)]
+    return [0.5 * sum(both[p][i] + half_silu(0.5 * terms[p][i]) for p in range(2)) for i in range(2)]
+
+
+def joined(mixed, sums, main, which):
+    def at(p, a, n):
+        return [x + y for x, y in zip(unpack(mixed[p, a : a + n], main, which), split(sums[p, a : a + n], main))]
+
+    return at
 
 
 def far_kernel(
-    main, flags, got, own, up, down, start, end, first, tails_first, second, tails_second, r_near, r_far, taps,
-    out, mixed, here, there, total, spread, edge_h, r, sums,
+    main, flags, got, own, up, down, start, end, first, tails_first, second, tails_second, r_far, taps, mixed,
+    out, here, total, spread, edge_h, r, sums,
 ):
     half = got.shape[0]
     cols = 2 * half
@@ -410,29 +440,24 @@
         return lambda k, g: [v[0] for v in split(ref[k * count + g : k * count + g + 1].astype(F32), main)]
 
     nearby = edge_stencil(flags, lambda g: at(own)(0, g), at(up), at(down), count, main, here, step)
-    inner_stencil(got_columns(got, main), lambda g: nearby[g], cols, count, here)
-    convolve(here, first, tails_first, total, 0, rows, main)
+    weave(inner_stencil(got_columns(got, main), lambda g: nearby[g], cols, count, here))
+    weave(convolve(here, first, tails_first, total, 0, rows, main))
     spread_halves(total, spread, cols, count, main, 0, step)
-    to_far, to_near = flags[TAP_FAR], flags[TAP_NEAR]
-    toward = [(to_far, to_near), (to_near, to_far)]
+    toward = [flags[TAP_FAR], flags[TAP_NEAR]]
     totals = second_convolution(
-        flags, spread, (start, end), cols, count, main, second, tails_second, edge_h, here, there, total
-    )
+        flags, spread, (start, end), cols, count, main, second, tails_second, edge_h, here, total
+    )
+
+    residual(got_columns(got, main), totals, cols, main, r, flags[HAS_FAR] > 0)
 
     @stage(flags)
     def _():
         for p in range(2):
-            mixed[p] = mix([(r_far, toward[p][0]), (r_near, 1)], taps, main, p)
-        residual(got_columns(got, main), totals, cols, main, r, flags[HAS_FAR] > 0)
-
-    @stage(flags)
-    def _():
-        for p in range(2):
-            sums[p] = mix([(r, toward[p][0]), (r_far, 1), (r_near, toward[p][1])], taps, main, p)
+            sums[p] = mix([(r, toward[p])], taps, main, p)
 
     piece = CHUNK * SUB
     for s in range(0, size, piece):
-        value = blend(r_far, lambda p, a, n: split(sums[p, a : a + n], main), s, piece, main)
+        value = blend(r_far, joined(mixed, sums, main, 0), s, piece, main)
         store(out, s // SUB, [v.reshape(CHUNK, SUB, v.shape[-1]) for v in value])
 
 
@@ -442,16 +467,14 @@
     copies[0].start()
     toward = [flags[TAP_NEAR], flags[TAP_FAR]]
     for p in range(2):
-        sums[p] = mixed[p] + mix([(got, toward[p])], taps, main, p)
+        sums[p] = mix([(got, toward[p])], taps, main, p)
     piece = CHUNK * SUB
     for i in range(parts):
         first, last = i * cols // parts, (i + 1) * cols // parts
 
-        @stage(flags)
-        def _():
-            for c in range(first, last, CHUNK):
-                value = blend(r_near, lambda p, a, n: split(sums[p, a : a + n], main), c * SUB, piece, main)
-                store(staged, c, [v.reshape(CHUNK, SUB, v.shape[-1]) for v in value])
+        for c in range(first, last, CHUNK):
+            value = blend(r_near, joined(mixed, sums, main, 1), c * SUB, piece, main)
+            store(staged, c, [v.reshape(CHUNK, SUB, v.shape[-1]) for v in value])
 
         copy = pltpu.make_async_copy(
             staged.at[first:last], out.at[flags[NEAR], first:last], sems.at[i]
@@ -504,7 +527,7 @@
     pixels, count = rows * cols, cols // 4
     step = pixels + PAD
     width = 3 * main + 2 * LANES
-    wide = main + 2 * LANES
+    wide = 2 * main + 2 * LANES
     packed = 2 * main + LANES
     frames_n, rows_n = lax.axis_size("frame"), lax.axis_size("row")
     frame, row = lax.axis_index("frame"), lax.axis_index("row")
@@ -517,9 +540,9 @@
     def struct(*shape, dtype=BF16):
         return jax.ShapeDtypeStruct(shape, dtype)
 
-    here, there = (step + (count + 3) * SUB, width), (step, width)
+    here = (2 * step + PAD, width)
     work = [
-        pltpu.VMEM(here, BF16), pltpu.VMEM(there, BF16), pltpu.VMEM((2 * step, wide), F32),
+        pltpu.VMEM(here, BF16), pltpu.VMEM((2 * step, wide), F32),
         pltpu.VMEM((cols + count, SUB, main + LANES), F32), pltpu.VMEM((2, count, SUB, main + LANES), F32),
     ]
     video, edge, sent = call(
@@ -533,24 +556,28 @@
     r_near, tails_first, tails_second = call(
         functools.partial(near_kernel, main),
         (struct(pixels, packed), struct(width, 2 * LANES), struct(width, 2 * LANES)),
-        (flags, video, edge, up, down, cond_start, cond_end, first, second), work, "near", 54 * unit,
+        (flags, video, edge, up, down, cond_start, cond_end, first, second), work, "near", 24 * unit,
     )
     got_near = lax.ppermute(r_near, "frame", pairs(frames_n, 0))
-    got_far, _ = lax.optimization_barrier((got_far, r_near))
-    far_edge = call(functools.partial(relay_kernel, main), struct(2 * count, SUB, main + LANES), (got_far,), name="relay")
-    far_up, far_down = row_neighbours(far_edge)
     r_far = call(
         functools.partial(other_kernel, main), struct(pixels, packed),
         (flags, video, edge, up, down, cond_start, cond_end, first, tails_first, second, tails_second),
-        work, "other", 54 * unit,
-    )
-    done, mixed = call(
-        functools.partial(far_kernel, main), (struct(cols, SUB, channels), struct(2, pixels, channels, dtype=F32)),
+        work, "other", 12 * unit,
+    )
+    got_far, r_far = lax.optimization_barrier((got_far, r_far))
+    far_edge = call(functools.partial(relay_kernel, main), struct(2 * count, SUB, main + LANES), (got_far,), name="relay")
+    far_up, far_down = row_neighbours(far_edge)
+    mixed = call(
+        functools.partial(mix_kernel, main), struct(2, pixels, packed, dtype=F32), (flags, r_near, r_far, taps),
+        name="mix", flops=2 * unit,
+    )
+    done = call(
+        functools.partial(far_kernel, main), struct(cols, SUB, channels),
         (
-            flags, got_far, far_edge, far_up, far_down, cond_start, cond_end, first, tails_first, second,
-            tails_second, r_near, r_far, taps,
+            flags, got_far, far_edge, far_up, far_down, cond_start, cond_end, first, tails_first, second, tails_second,
+            r_far, taps, mixed,
         ),
-        [*work, pltpu.VMEM((pixels, packed), BF16), pltpu.VMEM((2, pixels, channels), F32)], "far", 54 * unit,
+        [*work, pltpu.VMEM((pixels, packed), BF16), pltpu.VMEM((2, pixels, channels), F32)], "far", 12 * unit,
     )
     parts = 3
     out = call(

time: 25 us -> 24.6 us (0.984)
  the two profiles are of different devices: /device:TPU:15 before, /device:TPU:0 now
where the time goes in v3:
time: 24.6 us; the launch traced here: 24.4 us
  Pallas kernels  16.4 us (67%)
  starting transfers between devices  6.31 us (26%)
  local copies, waits for them, and re-layouts  1.12 us (5%)
  waiting for transfers between devices  0.44 us (2%)
    pallas_call x7, Pallas kernels, call(): pl.pallas_call(kernel, out_shape=outs, in_specs=[SMEM if a.dtype == jnp.i...  16.4 us
    ppermute x1, starting transfers between devices, shards(): got_near = lax.ppermute(r_near, 'frame', pairs(frames_n, 0))  5.02 us
    unnamed x12, local copies, waits for them, and re-layouts  1.03 us
    ppermute x1, starting transfers between devices, shards(): got_far = lax.ppermute(sent, 'frame', pairs(frames_n, 1))  0.66 us
    ppermute x2, starting transfers between devices, row_neighbours(): first = lax.ppermute(edge, 'row', pairs(count, 0))  0.63 us
  transfers between devices with their start and end apart: 4, of which 1 were waited for; matrix products, arithmetic and copies ran while one was open for 0% of the time, Pallas kernels for 56%

profile of v3, /device:TPU:0, one launch (start us, length us, event | category | flops | bytes accessed | tf_op | source)
XLA Modules:
  0.0 24.4 jit_solution(9672442758184446080)
XLA Ops:
  0.0 0.1 stack.43.flags
  0.1 0.0 copy-start.5
  0.1 1.0 %copy-done.5 = bf16[2,8,36,320]{3,1,2,0:T(8,128)(2,1)S(1)} copy-done((bf16[2,8,36,320]{3,1,2,0:T(8,128)(2,1)S(1)}, bf16[2,8,36,320]{3,1,2,0:T(8,128)(2,1)}, u32[]{:S(2)}) %copy-start.5) | copy-done | bytes 368664
  1.1 0.0 copy-start
  1.1 0.8 %prepare.1 = (bf16[2,36,8,384]{3,2,1,0:T(8,128)(2,1)S(1)}, bf16[36,8,384]{2,1,0:T(8,128)(2,1)S(1)}, bf16[18,8,640]{2,1,0:T(8,128)(2,1)S(1)}) custom-call(s32[7]{0:T(128)S(1)} %stack.43.flags, bf16[2,36,8,320]{3,2,1,0:T(8,128)(2,1)S(1)} %bitcast.9), custom_call_target="tpu_custom_call" | custom-call | flops 1207959552 | bytes 1048576 | tf_op jit(solution)/shard_map/prepare/pallas_call | solution.py:494
  1.9 0.6 %collective-permute-start = (bf16[36,8,384]{2,1,0:T(8,128)(2,1)S(1)}, bf16[36,8,384]{2,1,0:T(8,128)(2,1)S(1)}, u32[]{:S(2)}, u32[]{:S(2)}) collective-permute-start(bf16[36,8,384]{2,1,0:T(8,128)(2,1)S(1)} %get-tuple-element.14.own), channel_id=1, source_target_pairs={{0,1},{1,0},{2,3},{3,2},{4,5},{5,4},{6,7},{7,6},{8,9},{9,8},{10,11... | collective-permute-start | bytes 663560 | tf_op jit(solution)/shard_map/ppermute | solution.py:515
  2.5 0.7 %collective-permute-start.2 = (bf16[18,8,640]{2,1,0:T(8,128)(2,1)S(1)}, bf16[18,8,640]{2,1,0:T(8,128)(2,1)S(1)}, u32[]{:S(2)}, u32[]{:S(2)}) collective-permute-start(bf16[18,8,640]{2,1,0:T(8,128)(2,1)S(1)} %get-tuple-element.16), channel_id=1, source_target_pairs={{2,4},{6,8},{10,12},{14,16},{18,20},{22,24},{26,28},{4,2},{8,6},{1... | collective-permute-start | bytes 552968 | tf_op jit(solution)/shard_map/ppermute | solution.py:554
  3.2 0.4 %collective-permute-done.up.down = bf16[36,8,384]{2,1,0:T(8,128)(2,1)S(1)} collective-permute-done((bf16[36,8,384]{2,1,0:T(8,128)(2,1)S(1)}, bf16[36,8,384]{2,1,0:T(8,128)(2,1)S(1)}, u32[]{:S(2)}, u32[]{:S(2)}) %collective-permute-start) | collective-permute-done | bytes 221216 | tf_op jit(solution)/shard_map/ppermute | solution.py:515
  3.6 0.0 copy-done
  3.6 0.0 copy-done.1
  3.6 0.0 copy-done.3
  3.6 0.0 copy-done.4
  3.6 4.0 %near.1 = (bf16[288,640]{1,0:T(8,128)(2,1)S(1)}, bf16[1024,256]{1,0:T(8,128)(2,1)S(1)}, bf16[1024,256]{1,0:T(8,128)(2,1)S(1)}) custom-call(s32[7]{0:T(128)S(1)} %stack.43.flags, bf16[2,36,8,384]{3,2,1,0:T(8,128)(2,1)S(1)} %get-tuple-element.13.video, bf16[36,8,384]{2,1,0:T(8,128)(2,1)S(1)} %get-tuple-element.14.own, ...), custom_call_target="tpu_custom_call" | custom-call | flops 3623878656 | bytes 1048576 | tf_op jit(solution)/shard_map/near/pallas_call | solution.py:494
  7.6 5.0 %collective-permute-start.1 = (bf16[288,640]{1,0:T(8,128)(2,1)S(1)}, bf16[288,640]{1,0:T(8,128)(2,1)S(1)}, u32[]{:S(2)}, u32[]{:S(2)}) collective-permute-start(bf16[288,640]{1,0:T(8,128)(2,1)S(1)} %get-tuple-element.15.r_near), channel_id=1, source_target_pairs={{0,2},{4,6},{8,10},{12,14},{16,18},{20,22},{24,26},{28,30},{2,0},{... | collective-permute-start | bytes 1105928 | tf_op jit(solution)/shard_map/ppermute | solution.py:561
  12.7 3.9 %other.1.r_far = bf16[288,640]{1,0:T(8,128)(2,1)S(1)} custom-call(s32[7]{0:T(128)S(1)} %stack.43.flags, bf16[2,36,8,384]{3,2,1,0:T(8,128)(2,1)S(1)} %get-tuple-element.13.video, bf16[36,8,384]{2,1,0:T(8,128)(2,1)S(1)} %get-tuple-element.14.own, bf16[36,8,384]{2,1,0:T(8,128)(2,1)S(1)} %collective-permute-done.up.down, ...), custom_call_target="tpu_custom_call" | custom-call | flops 1811939328 | bytes 1048576 | tf_op jit(solution)/shard_map/other/pallas_call | solution.py:494
  16.5 0.0 collective-permute-done.2.got
  16.5 0.1 relay.1.own
  16.7 0.1 collective-permute-start.3
  16.7 0.0 copy-done.2
  16.7 1.4 %mix.1.mixed = f32[2,288,640]{2,1,0:T(8,128)S(1)} custom-call(s32[7]{0:T(128)S(1)} %stack.43.flags, bf16[288,640]{1,0:T(8,128)(2,1)S(1)} %get-tuple-element.15.r_near, bf16[288,640]{1,0:T(8,128)(2,1)S(1)} %other.1.r_far, bf16[3,320,320]{2,1,0:T(8,128)(2,1)S(1)} %copy-done.2), custom_call_target="tpu_custom_call" | custom-call | flops 301989888 | bytes 1048576 | tf_op jit(solution)/shard_map/mix/pallas_call | solution.py:494
  18.1 0.0 collective-permute-done.3.up.down
  18.2 4.4 %far.1.done = bf16[36,8,320]{2,1,0:T(8,128)(2,1)S(1)} custom-call(s32[7]{0:T(128)S(1)} %stack.43.flags, bf16[18,8,640]{2,1,0:T(8,128)(2,1)S(1)} %collective-permute-done.2.got, bf16[18,8,384]{2,1,0:T(8,128)(2,1)S(1)} %relay.1.own, bf16[18,8,384]{2,1,0:T(8,128)(2,1)S(1)} %collective-permute-done.3.up.down, ...), custom_call_target="tpu_custom_call" | custom-call | flops 1811939328 | bytes 1048576 | tf_op jit(solution)/shard_map/far/pallas_call | solution.py:494
  22.6 0.0 collective-permute-done.1.got
  22.6 1.8 %last.1 = bf16[2,36,8,320]{3,2,1,0:T(8,128)(2,1)} custom-call(s32[7]{0:T(128)S(1)} %stack.43.flags, bf16[288,640]{1,0:T(8,128)(2,1)S(1)} %collective-permute-done.1.got, f32[2,288,640]{2,1,0:T(8,128)S(1)} %mix.1.mixed, bf16[288,640]{1,0:T(8,128)(2,1)S(1)} %get-tuple-element.15.r_near, bf16[3,320,320]{2,1,0:T(8,128)(2,1)S(1)} %copy-done.2, ...), custom_call_target="tpu_custom_call" | custom-call | flops 603979776 | bytes 1048576 | tf_op jit(solution)/shard_map/last/pallas_call | solution.py:494
  (4 shorter events, 0.0 us)
Async XLA Ops:
  0.1 1.0 %copy-start.5 = (bf16[2,8,36,320]{3,1,2,0:T(8,128)(2,1)S(1)}, bf16[2,8,36,320]{3,1,2,0:T(8,128)(2,1)}, u32[]{:S(2)}) copy-start(bf16[2,8,36,320]{3,1,2,0:T(8,128)(2,1)} %param.6) | copy-start | bytes 1105924
  1.1 2.5 %copy-start = (bf16[3,3,320,320]{3,2,1,0:T(8,128)(2,1)S(1)}, bf16[3,3,320,320]{3,2,1,0:T(8,128)(2,1)}, u32[]{:S(2)}) copy-start(bf16[3,3,320,320]{3,2,1,0:T(8,128)(2,1)} %first.5) | copy-start | bytes 5529604
  1.1 2.5 %copy-start.1 = (bf16[3,3,320,320]{3,2,1,0:T(8,128)(2,1)S(1)}, bf16[3,3,320,320]{3,2,1,0:T(8,128)(2,1)}, u32[]{:S(2)}) copy-start(bf16[3,3,320,320]{3,2,1,0:T(8,128)(2,1)} %second.5) | copy-start | bytes 5529604
  1.1 2.5 %copy-start.3 = (f32[320]{0:T(512)S(1)}, f32[320]{0:T(512)}, u32[]{:S(2)}) copy-start(f32[320]{0:T(512)} %start.5) | copy-start | bytes 3844
  1.1 2.5 %copy-start.4 = (f32[320]{0:T(512)S(1)}, f32[320]{0:T(512)}, u32[]{:S(2)}) copy-start(f32[320]{0:T(512)} %end.5) | copy-start | bytes 3844
  1.9 1.7 %collective-permute-start = (bf16[36,8,384]{2,1,0:T(8,128)(2,1)S(1)}, bf16[36,8,384]{2,1,0:T(8,128)(2,1)S(1)}, u32[]{:S(2)}, u32[]{:S(2)}) collective-permute-start(bf16[36,8,384]{2,1,0:T(8,128)(2,1)S(1)} %get-tuple-element.14.own), channel_id=1, source_target_pairs={{0,1},{1,0},{2,3},{3,2},{4,5},{5,4},{6,7},{7,6},{8,9},{9,8},{10,11... | collective-permute-start | bytes 663560 | tf_op jit(solution)/shard_map/ppermute | solution.py:515
  2.5 14.0 %collective-permute-start.2 = (bf16[18,8,640]{2,1,0:T(8,128)(2,1)S(1)}, bf16[18,8,640]{2,1,0:T(8,128)(2,1)S(1)}, u32[]{:S(2)}, u32[]{:S(2)}) collective-permute-start(bf16[18,8,640]{2,1,0:T(8,128)(2,1)S(1)} %get-tuple-element.16), channel_id=1, source_target_pairs={{2,4},{6,8},{10,12},{14,16},{18,20},{22,24},{26,28},{4,2},{8,6},{1... | collective-permute-start | bytes 552968 | tf_op jit(solution)/shard_map/ppermute | solution.py:554
  7.6 14.9 %collective-permute-start.1 = (bf16[288,640]{1,0:T(8,128)(2,1)S(1)}, bf16[288,640]{1,0:T(8,128)(2,1)S(1)}, u32[]{:S(2)}, u32[]{:S(2)}) collective-permute-start(bf16[288,640]{1,0:T(8,128)(2,1)S(1)} %get-tuple-element.15.r_near), channel_id=1, source_target_pairs={{0,2},{4,6},{8,10},{12,14},{16,18},{20,22},{24,26},{28,30},{2,0},{... | collective-permute-start | bytes 1105928 | tf_op jit(solution)/shard_map/ppermute | solution.py:561
  12.7 4.1 %copy-start.2 = (bf16[3,320,320]{2,1,0:T(8,128)(2,1)S(1)}, bf16[3,320,320]{2,1,0:T(8,128)(2,1)}, u32[]{:S(2)}) copy-start(bf16[3,320,320]{2,1,0:T(8,128)(2,1)} %taps.5) | copy-start | bytes 1843204
  16.7 1.5 %collective-permute-start.3 = (bf16[18,8,384]{2,1,0:T(8,128)(2,1)S(1)}, bf16[18,8,384]{2,1,0:T(8,128)(2,1)S(1)}, u32[]{:S(2)}, u32[]{:S(2)}) collective-permute-start(bf16[18,8,384]{2,1,0:T(8,128)(2,1)S(1)} %relay.1.own), channel_id=1, source_target_pairs={{0,1},{1,0},{2,3},{3,2},{4,5},{5,4},{6,7},{7,6},{8,9},{9,8},{10,11... | collective-permute-start | bytes 331784 | tf_op jit(solution)/shard_map/ppermute | solution.py:515

commit v4 on v3

--- a/solution.py
+++ b/solution.py
@@ -62,15 +62,17 @@
     def tile(g):
         outer, second = None, None
         for j in range(4):
-            x = column(j * count + g)
-            z = [jnp.where(rows_of(v) == 7, turn(v, 1), turn(v, -1)) for v in x]
-            x, z = [turn(v, 2 * j) for v in x], [turn(v, 2 * j) for v in z]
-            if j == 0:
-                outer, second = x, z
-            else:
-                at = lambda v: (rows_of(v) == (2 * j + 7) % 8) | (rows_of(v) == 2 * j)
-                outer = [jnp.where(at(v), v, o) for v, o in zip(x, outer)]
-                second = [jnp.where(at(v), v, o) for v, o in zip(z, second)]
+            x = [turn(v, 2 * j) for v in column(j * count + g)]
+
+            def place(old, above, below):
+                if old is None:
+                    return x
+                return [
+                    jnp.where((rows_of(v) == (2 * j + above) % 8) | (rows_of(v) == (2 * j + below) % 8), v, o)
+                    for v, o in zip(x, old)
+                ]
+
+            outer, second = place(outer, 7, 0), place(second, 6, 1)
         return outer, second
 
     return tile
@@ -177,8 +179,8 @@
         for i in range(2):
             above = lax.rem(rows_of(own[i]), 2) == 1
             crossed = jnp.where(above, turn(own[i], -1), turn(own[i], 1))
-            u_out, u_sec = (jnp.where(has_up, ups[k][i], 0.0) for k in range(2))
-            d_out, d_sec = (jnp.where(has_down, downs[k][i], 0.0) for k in range(2))
+            u_out, u_sec = (jnp.where(has_up, turn(ups[k][i], k), 0.0) for k in range(2))
+            d_out, d_sec = (jnp.where(has_down, turn(downs[k][i], -k), 0.0) for k in range(2))
             prev.append(jnp.where(above, u_sec, crossed))
             mid.append(jnp.where(above, u_out, d_out))
             nxt.append(jnp.where(above, crossed, d_sec))
@@ -360,7 +362,7 @@
 
 def other_kernel(
     main, flags, video, own, up, down, start, end, first, tails_first, second, tails_second,
-    r, here, total, spread, edge_h,
+    total, here, spread, edge_h,
 ):
     cols = video.shape[1]
     count, step = cols // 4, cols * SUB + PAD
@@ -373,14 +375,11 @@
 
     spread_halves(total, spread, cols, count, main, 0, step)
 
-    totals = second_convolution(
-        flags, spread, (start, end), cols, count, main, second, tails_second, edge_h, here, total
-    )
-    residual(columns(video, flags[FAR], main), totals, cols, main, r)
-
-
-def mix(sources, taps, main, p):
-    left = [r[:, p * main : (p + 1) * main] for r, _ in sources] + [r[:, 2 * main :] for r, _ in sources]
+    second_convolution(flags, spread, (start, end), cols, count, main, second, tails_second, edge_h, here, total)
+
+
+def mix(sources, taps, main, p, rows=slice(None)):
+    left = [r[rows, p * main : (p + 1) * main] for r, _ in sources] + [r[rows, 2 * main :] for r, _ in sources]
     right = [taps[t, :main] for _, t in sources]
     for _, t in sources:
         tail = taps[t, main:]
@@ -388,27 +387,34 @@
     return jnp.dot(jnp.concatenate(left, axis=1), jnp.concatenate(right, axis=0), preferred_element_type=F32)
 
 
-def mix_kernel(main, flags, r_near, r_far, taps, mixed):
+def mix_kernel(main, flags, video, total, r_near, taps, r_far, mixed):
+    cols = video.shape[1]
     toward = [(flags[TAP_FAR], flags[TAP_NEAR]), (flags[TAP_NEAR], flags[TAP_FAR])]
+
+    def columns_of(a, b):
+        return [a[:, :main], b[:, :main], jnp.concatenate([a[:, main:], b[:, main:]], axis=1)]
+
+    def tails_of(p, a, b):
+        parts = columns_of(a[main:], b[main:])
+        blanks = [jnp.zeros_like(v) for v in parts]
+        return [jnp.concatenate(v, axis=0) for v in (zip(parts, blanks) if p == 0 else zip(blanks, parts))]
+
+    near = [
+        [
+            jnp.dot(r_near[:, p * main : (p + 1) * main], right, preferred_element_type=F32)
+            for right in columns_of(taps[toward[p][1], :main], taps[1, :main])
+        ]
+        for p in range(2)
+    ]
+    residual(columns(video, flags[FAR], main), [(total, 0), (total, cols * SUB + PAD)], cols, main, r_far)
     for p in range(2):
         to_far, to_near = toward[p]
-        left = [r[:, part] for part in (slice(p * main, (p + 1) * main), slice(2 * main, None)) for r in (r_far, r_near)]
-
-        pairs_of = [(taps[1], taps[to_far]), (taps[to_near], taps[1])]
-
-        def right(column):
-            parts = [column(a[:main], b[:main]) for a, b in pairs_of]
-            for tail in [column(a[main:], b[main:]) for a, b in pairs_of]:
-                blank = jnp.zeros_like(tail)
-                parts += [tail, blank] if p == 0 else [blank, tail]
-            return jnp.concatenate(parts, axis=0)
-
-        value = jnp.concatenate(left, axis=1)
-        columns_of = [
-            lambda a, b: a[:, :main], lambda a, b: b[:, :main], lambda a, b: jnp.concatenate([a[:, main:], b[:, main:]], axis=1)
-        ]
-        for k, column in enumerate(columns_of):
-            part = jnp.dot(value, right(column), preferred_element_type=F32)
+        left = jnp.concatenate([r_far[:, p * main : (p + 1) * main], r_far[:, 2 * main :], r_near[:, 2 * main :]], axis=1)
+        rights = zip(
+            columns_of(taps[1, :main], taps[to_far, :main]), tails_of(p, taps[1], taps[to_far]), tails_of(p, taps[to_near], taps[1])
+        )
+        for k, right in enumerate(rights):
+            part = near[p][k] + jnp.dot(left, jnp.concatenate(right, axis=0), preferred_element_type=F32)
             mixed[p, :, k * main : k * main + part.shape[1]] = part
 
 
@@ -466,12 +472,13 @@
     copies = [pltpu.make_async_copy(done, out.at[flags[FAR]], sems.at[parts])]
     copies[0].start()
     toward = [flags[TAP_NEAR], flags[TAP_FAR]]
-    for p in range(2):
-        sums[p] = mix([(got, toward[p])], taps, main, p)
-    piece = CHUNK * SUB
+    piece, halves = CHUNK * SUB, 2
     for i in range(parts):
         first, last = i * cols // parts, (i + 1) * cols // parts
-
+        if i % (parts // halves) == 0:
+            rows = slice(first * SUB, (first + cols // halves) * SUB)
+            for p in range(2):
+                sums[p, rows] = mix([(got, toward[p])], taps, main, p, rows)
         for c in range(first, last, CHUNK):
             value = blend(r_near, joined(mixed, sums, main, 1), c * SUB, piece, main)
             store(staged, c, [v.reshape(CHUNK, SUB, v.shape[-1]) for v in value])
@@ -559,16 +566,17 @@
         (flags, video, edge, up, down, cond_start, cond_end, first, second), work, "near", 24 * unit,
     )
     got_near = lax.ppermute(r_near, "frame", pairs(frames_n, 0))
-    r_far = call(
-        functools.partial(other_kernel, main), struct(pixels, packed),
+    total_far = call(
+        functools.partial(other_kernel, main), struct(2 * step, wide, dtype=F32),
         (flags, video, edge, up, down, cond_start, cond_end, first, tails_first, second, tails_second),
-        work, "other", 12 * unit,
-    )
-    got_far, r_far = lax.optimization_barrier((got_far, r_far))
+        [work[0], *work[2:]], "other", 12 * unit,
+    )
+    got_far, total_far = lax.optimization_barrier((got_far, total_far))
     far_edge = call(functools.partial(relay_kernel, main), struct(2 * count, SUB, main + LANES), (got_far,), name="relay")
     far_up, far_down = row_neighbours(far_edge)
-    mixed = call(
-        functools.partial(mix_kernel, main), struct(2, pixels, packed, dtype=F32), (flags, r_near, r_far, taps),
+    r_far, mixed = call(
+        functools.partial(mix_kernel, main), (struct(pixels, packed), struct(2, pixels, packed, dtype=F32)),
+        (flags, video, total_far, r_near, taps),
         name="mix", flops=2 * unit,
     )
     done = call(
@@ -579,7 +587,7 @@
         ),
         [*work, pltpu.VMEM((pixels, packed), BF16), pltpu.VMEM((2, pixels, channels), F32)], "far", 12 * unit,
     )
-    parts = 3
+    parts = 6
     out = call(
         functools.partial(last_kernel, main, parts), struct(2, cols, SUB, channels),
         (flags, got_near, mixed, r_near, taps, done),

time: 24.6 us -> 24.4 us (level)
  transfers between devices with their start and end apart: 4 -> 4, of which waited for: 1 -> 1; matrix products, arithmetic and copies ran while one was open for 0% -> 0% of each run, Pallas kernels for 56% -> 57%
where the time goes in v4:
time: 24.4 us; the launch traced here: 24.2 us
  Pallas kernels  16.2 us (66%)
  starting transfers between devices  6.44 us (26%)
  local copies, waits for them, and re-layouts  1.12 us (5%)
  waiting for transfers between devices  0.31 us (1%)
    pallas_call x7, Pallas kernels, call(): pl.pallas_call(kernel, out_shape=outs, in_specs=[SMEM if a.dtype == jnp.i...  16.2 us
    ppermute x1, starting transfers between devices, shards(): got_near = lax.ppermute(r_near, 'frame', pairs(frames_n, 0))  5.02 us
    unnamed x12, local copies, waits for them, and re-layouts  1.03 us
    ppermute x1, starting transfers between devices, shards(): got_far = lax.ppermute(sent, 'frame', pairs(frames_n, 1))  0.79 us
    ppermute x2, starting transfers between devices, row_neighbours(): first = lax.ppermute(edge, 'row', pairs(count, 0))  0.63 us
  transfers between devices with their start and end apart: 4, of which 1 were waited for; matrix products, arithmetic and copies ran while one was open for 0% of the time, Pallas kernels for 57%

profile of v4, /device:TPU:0, one launch (start us, length us, event | category | flops | bytes accessed | tf_op | source)
XLA Modules:
  0.0 24.2 jit_solution(16978607916243441830)
XLA Ops:
  0.0 0.1 stack.43.flags
  0.1 0.0 copy-start.5
  0.1 1.0 %copy-done.5 = bf16[2,8,36,320]{3,1,2,0:T(8,128)(2,1)S(1)} copy-done((bf16[2,8,36,320]{3,1,2,0:T(8,128)(2,1)S(1)}, bf16[2,8,36,320]{3,1,2,0:T(8,128)(2,1)}, u32[]{:S(2)}) %copy-start.5) | copy-done | bytes 368664
  1.1 0.0 copy-start
  1.1 0.7 %prepare.1 = (bf16[2,36,8,384]{3,2,1,0:T(8,128)(2,1)S(1)}, bf16[36,8,384]{2,1,0:T(8,128)(2,1)S(1)}, bf16[18,8,640]{2,1,0:T(8,128)(2,1)S(1)}) custom-call(s32[7]{0:T(128)S(1)} %stack.43.flags, bf16[2,36,8,320]{3,2,1,0:T(8,128)(2,1)S(1)} %bitcast.9), custom_call_target="tpu_custom_call" | custom-call | flops 1207959552 | bytes 1048576 | tf_op jit(solution)/shard_map/prepare/pallas_call | solution.py:501
  1.8 0.6 %collective-permute-start = (bf16[36,8,384]{2,1,0:T(8,128)(2,1)S(1)}, bf16[36,8,384]{2,1,0:T(8,128)(2,1)S(1)}, u32[]{:S(2)}, u32[]{:S(2)}) collective-permute-start(bf16[36,8,384]{2,1,0:T(8,128)(2,1)S(1)} %get-tuple-element.16.own), channel_id=1, source_target_pairs={{0,1},{1,0},{2,3},{3,2},{4,5},{5,4},{6,7},{7,6},{8,9},{9,8},{10,11... | collective-permute-start | bytes 663560 | tf_op jit(solution)/shard_map/ppermute | solution.py:522
  2.4 0.8 %collective-permute-start.2 = (bf16[18,8,640]{2,1,0:T(8,128)(2,1)S(1)}, bf16[18,8,640]{2,1,0:T(8,128)(2,1)S(1)}, u32[]{:S(2)}, u32[]{:S(2)}) collective-permute-start(bf16[18,8,640]{2,1,0:T(8,128)(2,1)S(1)} %get-tuple-element.18), channel_id=1, source_target_pairs={{2,4},{6,8},{10,12},{14,16},{18,20},{22,24},{26,28},{4,2},{8,6},{1... | collective-permute-start | bytes 552968 | tf_op jit(solution)/shard_map/ppermute | solution.py:561
  3.2 0.3 %collective-permute-done.up.down = bf16[36,8,384]{2,1,0:T(8,128)(2,1)S(1)} collective-permute-done((bf16[36,8,384]{2,1,0:T(8,128)(2,1)S(1)}, bf16[36,8,384]{2,1,0:T(8,128)(2,1)S(1)}, u32[]{:S(2)}, u32[]{:S(2)}) %collective-permute-start) | collective-permute-done | bytes 221216 | tf_op jit(solution)/shard_map/ppermute | solution.py:522
  3.5 0.0 copy-done
  3.5 0.0 copy-done.1
  3.5 0.0 copy-done.3
  3.5 0.0 copy-done.4
  3.5 4.0 %near.1 = (bf16[288,640]{1,0:T(8,128)(2,1)S(1)}, bf16[1024,256]{1,0:T(8,128)(2,1)S(1)}, bf16[1024,256]{1,0:T(8,128)(2,1)S(1)}) custom-call(s32[7]{0:T(128)S(1)} %stack.43.flags, bf16[2,36,8,384]{3,2,1,0:T(8,128)(2,1)S(1)} %get-tuple-element.15.video, bf16[36,8,384]{2,1,0:T(8,128)(2,1)S(1)} %get-tuple-element.16.own, ...), custom_call_target="tpu_custom_call" | custom-call | flops 3623878656 | bytes 1048576 | tf_op jit(solution)/shard_map/near/pallas_call | solution.py:501
  7.5 5.0 %collective-permute-start.1 = (bf16[288,640]{1,0:T(8,128)(2,1)S(1)}, bf16[288,640]{1,0:T(8,128)(2,1)S(1)}, u32[]{:S(2)}, u32[]{:S(2)}) collective-permute-start(bf16[288,640]{1,0:T(8,128)(2,1)S(1)} %get-tuple-element.17.r_near), channel_id=1, source_target_pairs={{0,2},{4,6},{8,10},{12,14},{16,18},{20,22},{24,26},{28,30},{2,0},{... | collective-permute-start | bytes 1105928 | tf_op jit(solution)/shard_map/ppermute | solution.py:568
  12.6 3.6 %other.1.total = f32[608,768]{1,0:T(8,128)S(1)} custom-call(s32[7]{0:T(128)S(1)} %stack.43.flags, bf16[2,36,8,384]{3,2,1,0:T(8,128)(2,1)S(1)} %get-tuple-element.15.video, bf16[36,8,384]{2,1,0:T(8,128)(2,1)S(1)} %get-tuple-element.16.own, bf16[36,8,384]{2,1,0:T(8,128)(2,1)S(1)} %collective-permute-done.up.down, ...), custom_call_target="tpu_custom_call" | custom-call | flops 1811939328 | bytes 1048576 | tf_op jit(solution)/shard_map/other/pallas_call | solution.py:501
  16.2 0.0 collective-permute-done.2.got
  16.2 0.1 relay.1.own
  16.3 0.1 collective-permute-start.3
  16.4 0.0 copy-done.2
  16.4 1.6 %mix.1 = (bf16[288,640]{1,0:T(8,128)(2,1)S(1)}, f32[2,288,640]{2,1,0:T(8,128)S(1)}) custom-call(s32[7]{0:T(128)S(1)} %stack.43.flags, bf16[2,36,8,384]{3,2,1,0:T(8,128)(2,1)S(1)} %get-tuple-element.15.video, f32[608,768]{1,0:T(8,128)S(1)} %other.1.total, bf16[288,640]{1,0:T(8,128)(2,1)S(1)} %get-tuple-element.17.r_near, bf16[3,320,320]{2,1,0:T(8,128)(2,1)S(1)} %copy-done.2), custom_call_target="tpu_custom_call" | custom-call | flops 301989888 | bytes 1048576 | tf_op jit(solution)/shard_map/mix/pallas_call | solution.py:501
  18.0 0.0 collective-permute-done.3.up.down
  18.0 4.4 %far.1.done = bf16[36,8,320]{2,1,0:T(8,128)(2,1)S(1)} custom-call(s32[7]{0:T(128)S(1)} %stack.43.flags, bf16[18,8,640]{2,1,0:T(8,128)(2,1)S(1)} %collective-permute-done.2.got, bf16[18,8,384]{2,1,0:T(8,128)(2,1)S(1)} %relay.1.own, bf16[18,8,384]{2,1,0:T(8,128)(2,1)S(1)} %collective-permute-done.3.up.down, ...), custom_call_target="tpu_custom_call" | custom-call | flops 1811939328 | bytes 1048576 | tf_op jit(solution)/shard_map/far/pallas_call | solution.py:501
  22.4 0.0 collective-permute-done.1.got
  22.4 1.8 %last.1 = bf16[2,36,8,320]{3,2,1,0:T(8,128)(2,1)} custom-call(s32[7]{0:T(128)S(1)} %stack.43.flags, bf16[288,640]{1,0:T(8,128)(2,1)S(1)} %collective-permute-done.1.got, f32[2,288,640]{2,1,0:T(8,128)S(1)} %get-tuple-element.22.mixed, bf16[288,640]{1,0:T(8,128)(2,1)S(1)} %get-tuple-element.17.r_near, bf16[3,320,320]{2,1,0:T(8,128)(2,1)S(1)} %copy-done.2, ...), custom_call_target="tpu_custom_call" | custom-call | flops 603979776 | bytes 1048576 | tf_op jit(solution)/shard_map/last/pallas_call | solution.py:501
  (4 shorter events, 0.0 us)
Async XLA Ops:
  0.1 1.0 %copy-start.5 = (bf16[2,8,36,320]{3,1,2,0:T(8,128)(2,1)S(1)}, bf16[2,8,36,320]{3,1,2,0:T(8,128)(2,1)}, u32[]{:S(2)}) copy-start(bf16[2,8,36,320]{3,1,2,0:T(8,128)(2,1)} %param.6) | copy-start | bytes 1105924
  1.1 2.4 %copy-start = (bf16[3,3,320,320]{3,2,1,0:T(8,128)(2,1)S(1)}, bf16[3,3,320,320]{3,2,1,0:T(8,128)(2,1)}, u32[]{:S(2)}) copy-start(bf16[3,3,320,320]{3,2,1,0:T(8,128)(2,1)} %first.5) | copy-start | bytes 5529604
  1.1 2.4 %copy-start.1 = (bf16[3,3,320,320]{3,2,1,0:T(8,128)(2,1)S(1)}, bf16[3,3,320,320]{3,2,1,0:T(8,128)(2,1)}, u32[]{:S(2)}) copy-start(bf16[3,3,320,320]{3,2,1,0:T(8,128)(2,1)} %second.5) | copy-start | bytes 5529604
  1.1 2.4 %copy-start.3 = (f32[320]{0:T(512)S(1)}, f32[320]{0:T(512)}, u32[]{:S(2)}) copy-start(f32[320]{0:T(512)} %start.5) | copy-start | bytes 3844
  1.1 2.4 %copy-start.4 = (f32[320]{0:T(512)S(1)}, f32[320]{0:T(512)}, u32[]{:S(2)}) copy-start(f32[320]{0:T(512)} %end.5) | copy-start | bytes 3844
  1.8 1.7 %collective-permute-start = (bf16[36,8,384]{2,1,0:T(8,128)(2,1)S(1)}, bf16[36,8,384]{2,1,0:T(8,128)(2,1)S(1)}, u32[]{:S(2)}, u32[]{:S(2)}) collective-permute-start(bf16[36,8,384]{2,1,0:T(8,128)(2,1)S(1)} %get-tuple-element.16.own), channel_id=1, source_target_pairs={{0,1},{1,0},{2,3},{3,2},{4,5},{5,4},{6,7},{7,6},{8,9},{9,8},{10,11... | collective-permute-start | bytes 663560 | tf_op jit(solution)/shard_map/ppermute | solution.py:522
  2.4 13.8 %collective-permute-start.2 = (bf16[18,8,640]{2,1,0:T(8,128)(2,1)S(1)}, bf16[18,8,640]{2,1,0:T(8,128)(2,1)S(1)}, u32[]{:S(2)}, u32[]{:S(2)}) collective-permute-start(bf16[18,8,640]{2,1,0:T(8,128)(2,1)S(1)} %get-tuple-element.18), channel_id=1, source_target_pairs={{2,4},{6,8},{10,12},{14,16},{18,20},{22,24},{26,28},{4,2},{8,6},{1... | collective-permute-start | bytes 552968 | tf_op jit(solution)/shard_map/ppermute | solution.py:561
  7.5 14.8 %collective-permute-start.1 = (bf16[288,640]{1,0:T(8,128)(2,1)S(1)}, bf16[288,640]{1,0:T(8,128)(2,1)S(1)}, u32[]{:S(2)}, u32[]{:S(2)}) collective-permute-start(bf16[288,640]{1,0:T(8,128)(2,1)S(1)} %get-tuple-element.17.r_near), channel_id=1, source_target_pairs={{0,2},{4,6},{8,10},{12,14},{16,18},{20,22},{24,26},{28,30},{2,0},{... | collective-permute-start | bytes 1105928 | tf_op jit(solution)/shard_map/ppermute | solution.py:568
  12.5 3.8 %copy-start.2 = (bf16[3,320,320]{2,1,0:T(8,128)(2,1)S(1)}, bf16[3,320,320]{2,1,0:T(8,128)(2,1)}, u32[]{:S(2)}) copy-start(bf16[3,320,320]{2,1,0:T(8,128)(2,1)} %taps.5) | copy-start | bytes 1843204
  16.3 1.7 %collective-permute-start.3 = (bf16[18,8,384]{2,1,0:T(8,128)(2,1)S(1)}, bf16[18,8,384]{2,1,0:T(8,128)(2,1)S(1)}, u32[]{:S(2)}, u32[]{:S(2)}) collective-permute-start(bf16[18,8,384]{2,1,0:T(8,128)(2,1)S(1)} %relay.1.own), channel_id=1, source_target_pairs={{0,1},{1,0},{2,3},{3,2},{4,5},{5,4},{6,7},{7,6},{8,9},{9,8},{10,11... | collective-permute-start | bytes 331784 | tf_op jit(solution)/shard_map/ppermute | solution.py:522

commit v5 on v4

--- a/solution.py
+++ b/solution.py
@@ -456,10 +456,8 @@
 
     residual(got_columns(got, main), totals, cols, main, r, flags[HAS_FAR] > 0)
 
-    @stage(flags)
-    def _():
-        for p in range(2):
-            sums[p] = mix([(r, toward[p])], taps, main, p)
+    for p in range(2):
+        sums[p] = mix([(r, toward[p])], taps, main, p)
 
     piece = CHUNK * SUB
     for s in range(0, size, piece):

time: 24.4 us -> 24 us (0.984)
  Pallas kernels: 16.2 us -> 15.9 us
    pallas_call x7, Pallas kernels: 16.2 us -> 15.9 us  [call(): pl.pallas_call(kernel, out_shape=outs, in_specs=[SMEM if a.dtype == jnp.i...]
  transfers between devices with their start and end apart: 4 -> 4, of which waited for: 1 -> 1; matrix products, arithmetic and copies ran while one was open for 0% -> 0% of each run, Pallas kernels for 57% -> 56%
where the time goes in v5:
time: 24 us; the launch traced here: 23.8 us
  Pallas kernels  15.9 us (66%)
  starting transfers between devices  6.44 us (27%)
  local copies, waits for them, and re-layouts  1.12 us (5%)
  waiting for transfers between devices  0.31 us (1%)
    pallas_call x7, Pallas kernels, call(): pl.pallas_call(kernel, out_shape=outs, in_specs=[SMEM if a.dtype == jnp.i...  15.9 us
    ppermute x1, starting transfers between devices, shards(): got_near = lax.ppermute(r_near, 'frame', pairs(frames_n, 0))  5.02 us
    unnamed x12, local copies, waits for them, and re-layouts  1.03 us
    ppermute x1, starting transfers between devices, shards(): got_far = lax.ppermute(sent, 'frame', pairs(frames_n, 1))  0.79 us
    ppermute x2, starting transfers between devices, row_neighbours(): first = lax.ppermute(edge, 'row', pairs(count, 0))  0.63 us
  transfers between devices with their start and end apart: 4, of which 1 were waited for; matrix products, arithmetic and copies ran while one was open for 0% of the time, Pallas kernels for 56%

profile of v5, /device:TPU:0, one launch (start us, length us, event | category | flops | bytes accessed | tf_op | source)
XLA Modules:
  0.0 23.8 jit_solution(6839368737695184520)
XLA Ops:
  0.0 0.1 stack.43.flags
  0.1 0.0 copy-start.5
  0.1 1.0 %copy-done.5 = bf16[2,8,36,320]{3,1,2,0:T(8,128)(2,1)S(1)} copy-done((bf16[2,8,36,320]{3,1,2,0:T(8,128)(2,1)S(1)}, bf16[2,8,36,320]{3,1,2,0:T(8,128)(2,1)}, u32[]{:S(2)}) %copy-start.5) | copy-done | bytes 368664
  1.1 0.0 copy-start
  1.1 0.7 %prepare.1 = (bf16[2,36,8,384]{3,2,1,0:T(8,128)(2,1)S(1)}, bf16[36,8,384]{2,1,0:T(8,128)(2,1)S(1)}, bf16[18,8,640]{2,1,0:T(8,128)(2,1)S(1)}) custom-call(s32[7]{0:T(128)S(1)} %stack.43.flags, bf16[2,36,8,320]{3,2,1,0:T(8,128)(2,1)S(1)} %bitcast.9), custom_call_target="tpu_custom_call" | custom-call | flops 1207959552 | bytes 1048576 | tf_op jit(solution)/shard_map/prepare/pallas_call | solution.py:499
  1.8 0.6 %collective-permute-start = (bf16[36,8,384]{2,1,0:T(8,128)(2,1)S(1)}, bf16[36,8,384]{2,1,0:T(8,128)(2,1)S(1)}, u32[]{:S(2)}, u32[]{:S(2)}) collective-permute-start(bf16[36,8,384]{2,1,0:T(8,128)(2,1)S(1)} %get-tuple-element.16.own), channel_id=1, source_target_pairs={{0,1},{1,0},{2,3},{3,2},{4,5},{5,4},{6,7},{7,6},{8,9},{9,8},{10,11... | collective-permute-start | bytes 663560 | tf_op jit(solution)/shard_map/ppermute | solution.py:520
  2.4 0.8 %collective-permute-start.2 = (bf16[18,8,640]{2,1,0:T(8,128)(2,1)S(1)}, bf16[18,8,640]{2,1,0:T(8,128)(2,1)S(1)}, u32[]{:S(2)}, u32[]{:S(2)}) collective-permute-start(bf16[18,8,640]{2,1,0:T(8,128)(2,1)S(1)} %get-tuple-element.18), channel_id=1, source_target_pairs={{2,4},{6,8},{10,12},{14,16},{18,20},{22,24},{26,28},{4,2},{8,6},{1... | collective-permute-start | bytes 552968 | tf_op jit(solution)/shard_map/ppermute | solution.py:559
  3.2 0.3 %collective-permute-done.up.down = bf16[36,8,384]{2,1,0:T(8,128)(2,1)S(1)} collective-permute-done((bf16[36,8,384]{2,1,0:T(8,128)(2,1)S(1)}, bf16[36,8,384]{2,1,0:T(8,128)(2,1)S(1)}, u32[]{:S(2)}, u32[]{:S(2)}) %collective-permute-start) | collective-permute-done | bytes 221216 | tf_op jit(solution)/shard_map/ppermute | solution.py:520
  3.5 0.0 copy-done
  3.5 0.0 copy-done.1
  3.5 0.0 copy-done.3
  3.5 0.0 copy-done.4
  3.5 4.0 %near.1 = (bf16[288,640]{1,0:T(8,128)(2,1)S(1)}, bf16[1024,256]{1,0:T(8,128)(2,1)S(1)}, bf16[1024,256]{1,0:T(8,128)(2,1)S(1)}) custom-call(s32[7]{0:T(128)S(1)} %stack.43.flags, bf16[2,36,8,384]{3,2,1,0:T(8,128)(2,1)S(1)} %get-tuple-element.15.video, bf16[36,8,384]{2,1,0:T(8,128)(2,1)S(1)} %get-tuple-element.16.own, ...), custom_call_target="tpu_custom_call" | custom-call | flops 3623878656 | bytes 1048576 | tf_op jit(solution)/shard_map/near/pallas_call | solution.py:499
  7.5 5.0 %collective-permute-start.1 = (bf16[288,640]{1,0:T(8,128)(2,1)S(1)}, bf16[288,640]{1,0:T(8,128)(2,1)S(1)}, u32[]{:S(2)}, u32[]{:S(2)}) collective-permute-start(bf16[288,640]{1,0:T(8,128)(2,1)S(1)} %get-tuple-element.17.r_near), channel_id=1, source_target_pairs={{0,2},{4,6},{8,10},{12,14},{16,18},{20,22},{24,26},{28,30},{2,0},{... | collective-permute-start | bytes 1105928 | tf_op jit(solution)/shard_map/ppermute | solution.py:566
  12.6 3.6 %other.1.total = f32[608,768]{1,0:T(8,128)S(1)} custom-call(s32[7]{0:T(128)S(1)} %stack.43.flags, bf16[2,36,8,384]{3,2,1,0:T(8,128)(2,1)S(1)} %get-tuple-element.15.video, bf16[36,8,384]{2,1,0:T(8,128)(2,1)S(1)} %get-tuple-element.16.own, bf16[36,8,384]{2,1,0:T(8,128)(2,1)S(1)} %collective-permute-done.up.down, ...), custom_call_target="tpu_custom_call" | custom-call | flops 1811939328 | bytes 1048576 | tf_op jit(solution)/shard_map/other/pallas_call | solution.py:499
  16.2 0.0 collective-permute-done.2.got
  16.2 0.1 relay.1.own
  16.3 0.1 collective-permute-start.3
  16.4 0.0 copy-done.2
  16.4 1.6 %mix.1 = (bf16[288,640]{1,0:T(8,128)(2,1)S(1)}, f32[2,288,640]{2,1,0:T(8,128)S(1)}) custom-call(s32[7]{0:T(128)S(1)} %stack.43.flags, bf16[2,36,8,384]{3,2,1,0:T(8,128)(2,1)S(1)} %get-tuple-element.15.video, f32[608,768]{1,0:T(8,128)S(1)} %other.1.total, bf16[288,640]{1,0:T(8,128)(2,1)S(1)} %get-tuple-element.17.r_near, bf16[3,320,320]{2,1,0:T(8,128)(2,1)S(1)} %copy-done.2), custom_call_target="tpu_custom_call" | custom-call | flops 301989888 | bytes 1048576 | tf_op jit(solution)/shard_map/mix/pallas_call | solution.py:499
  18.0 0.0 collective-permute-done.3.up.down
  18.0 4.0 %far.1.done = bf16[36,8,320]{2,1,0:T(8,128)(2,1)S(1)} custom-call(s32[7]{0:T(128)S(1)} %stack.43.flags, bf16[18,8,640]{2,1,0:T(8,128)(2,1)S(1)} %collective-permute-done.2.got, bf16[18,8,384]{2,1,0:T(8,128)(2,1)S(1)} %relay.1.own, bf16[18,8,384]{2,1,0:T(8,128)(2,1)S(1)} %collective-permute-done.3.up.down, ...), custom_call_target="tpu_custom_call" | custom-call | flops 1811939328 | bytes 1048576 | tf_op jit(solution)/shard_map/far/pallas_call | solution.py:499
  22.0 0.0 collective-permute-done.1.got
  22.0 1.8 %last.1 = bf16[2,36,8,320]{3,2,1,0:T(8,128)(2,1)} custom-call(s32[7]{0:T(128)S(1)} %stack.43.flags, bf16[288,640]{1,0:T(8,128)(2,1)S(1)} %collective-permute-done.1.got, f32[2,288,640]{2,1,0:T(8,128)S(1)} %get-tuple-element.22.mixed, bf16[288,640]{1,0:T(8,128)(2,1)S(1)} %get-tuple-element.17.r_near, bf16[3,320,320]{2,1,0:T(8,128)(2,1)S(1)} %copy-done.2, ...), custom_call_target="tpu_custom_call" | custom-call | flops 603979776 | bytes 1048576 | tf_op jit(solution)/shard_map/last/pallas_call | solution.py:499
  (4 shorter events, 0.0 us)
Async XLA Ops:
  0.1 1.0 %copy-start.5 = (bf16[2,8,36,320]{3,1,2,0:T(8,128)(2,1)S(1)}, bf16[2,8,36,320]{3,1,2,0:T(8,128)(2,1)}, u32[]{:S(2)}) copy-start(bf16[2,8,36,320]{3,1,2,0:T(8,128)(2,1)} %param.6) | copy-start | bytes 1105924
  1.1 2.4 %copy-start = (bf16[3,3,320,320]{3,2,1,0:T(8,128)(2,1)S(1)}, bf16[3,3,320,320]{3,2,1,0:T(8,128)(2,1)}, u32[]{:S(2)}) copy-start(bf16[3,3,320,320]{3,2,1,0:T(8,128)(2,1)} %first.5) | copy-start | bytes 5529604
  1.1 2.4 %copy-start.1 = (bf16[3,3,320,320]{3,2,1,0:T(8,128)(2,1)S(1)}, bf16[3,3,320,320]{3,2,1,0:T(8,128)(2,1)}, u32[]{:S(2)}) copy-start(bf16[3,3,320,320]{3,2,1,0:T(8,128)(2,1)} %second.5) | copy-start | bytes 5529604
  1.1 2.4 %copy-start.3 = (f32[320]{0:T(512)S(1)}, f32[320]{0:T(512)}, u32[]{:S(2)}) copy-start(f32[320]{0:T(512)} %start.5) | copy-start | bytes 3844
  1.1 2.4 %copy-start.4 = (f32[320]{0:T(512)S(1)}, f32[320]{0:T(512)}, u32[]{:S(2)}) copy-start(f32[320]{0:T(512)} %end.5) | copy-start | bytes 3844
  1.8 1.7 %collective-permute-start = (bf16[36,8,384]{2,1,0:T(8,128)(2,1)S(1)}, bf16[36,8,384]{2,1,0:T(8,128)(2,1)S(1)}, u32[]{:S(2)}, u32[]{:S(2)}) collective-permute-start(bf16[36,8,384]{2,1,0:T(8,128)(2,1)S(1)} %get-tuple-element.16.own), channel_id=1, source_target_pairs={{0,1},{1,0},{2,3},{3,2},{4,5},{5,4},{6,7},{7,6},{8,9},{9,8},{10,11... | collective-permute-start | bytes 663560 | tf_op jit(solution)/shard_map/ppermute | solution.py:520
  2.4 13.8 %collective-permute-start.2 = (bf16[18,8,640]{2,1,0:T(8,128)(2,1)S(1)}, bf16[18,8,640]{2,1,0:T(8,128)(2,1)S(1)}, u32[]{:S(2)}, u32[]{:S(2)}) collective-permute-start(bf16[18,8,640]{2,1,0:T(8,128)(2,1)S(1)} %get-tuple-element.18), channel_id=1, source_target_pairs={{2,4},{6,8},{10,12},{14,16},{18,20},{22,24},{26,28},{4,2},{8,6},{1... | collective-permute-start | bytes 552968 | tf_op jit(solution)/shard_map/ppermute | solution.py:559
  7.5 14.5 %collective-permute-start.1 = (bf16[288,640]{1,0:T(8,128)(2,1)S(1)}, bf16[288,640]{1,0:T(8,128)(2,1)S(1)}, u32[]{:S(2)}, u32[]{:S(2)}) collective-permute-start(bf16[288,640]{1,0:T(8,128)(2,1)S(1)} %get-tuple-element.17.r_near), channel_id=1, source_target_pairs={{0,2},{4,6},{8,10},{12,14},{16,18},{20,22},{24,26},{28,30},{2,0},{... | collective-permute-start | bytes 1105928 | tf_op jit(solution)/shard_map/ppermute | solution.py:566
  12.5 3.8 %copy-start.2 = (bf16[3,320,320]{2,1,0:T(8,128)(2,1)S(1)}, bf16[3,320,320]{2,1,0:T(8,128)(2,1)}, u32[]{:S(2)}) copy-start(bf16[3,320,320]{2,1,0:T(8,128)(2,1)} %taps.5) | copy-start | bytes 1843204
  16.3 1.7 %collective-permute-start.3 = (bf16[18,8,384]{2,1,0:T(8,128)(2,1)S(1)}, bf16[18,8,384]{2,1,0:T(8,128)(2,1)S(1)}, u32[]{:S(2)}, u32[]{:S(2)}) collective-permute-start(bf16[18,8,384]{2,1,0:T(8,128)(2,1)S(1)} %relay.1.own), channel_id=1, source_target_pairs={{0,1},{1,0},{2,3},{3,2},{4,5},{5,4},{6,7},{7,6},{8,9},{9,8},{10,11... | collective-permute-start | bytes 331784 | tf_op jit(solution)/shard_map/ppermute | solution.py:520
